TPU v7x, 512 devices: a whole 4x4x16 slice. The times are simulated.
512 devices in a mesh: sp: 8 (over z_lo, core), dp: 64 (over z_hi, y, x).
Axes of the slice: x: 4, y: 4, z: 16 (z_hi: 4, z_lo: 4; z = z_hi * 4 + z_lo), core: 2. Of those that a mesh axis runs over, the one named last changes fastest.
Arguments:
- inputs: bfloat16 [512, 8, 8, 8, 128], P('dp', 'sp'), may hold values from -16 to 16
- cotangent: bfloat16 [512, 8, 8, 8, 128], P('dp', 'sp'), may hold values from -6 to 6
- w_conv: bfloat16 [3456, 128], replicated, may hold values from -0.109375 to 0.109375
- w_down: bfloat16 [1024, 256], replicated, may hold values from -0.1875 to 0.1875
- w_up: bfloat16 [2048, 128], replicated, may hold values from -0.375 to 0.375
Outputs:
- grad_input: bfloat16 [512, 8, 8, 8, 128], P('dp', 'sp')
- weight_grads: float32 [966656], P('dp')
All inputs are finite; a program needn't handle non-finite values.
Results may differ from a plain program's by a relative error of at most 0.017.
Values may be sent and summed in bfloat16 or wider, within the bound.
A program may use at most 64 MiB of HBM per device.

v0:
```python
import jax
import jax.numpy as jnp
from jax import lax
from jax.sharding import PartitionSpec as P


def extended(cells, sides, width):
    for axis, dim in sides:
        count = lax.axis_size(axis)
        ends = count - 1
        head = lax.slice_in_dim(cells, 0, width, axis=dim)
        tail = lax.slice_in_dim(cells, cells.shape[dim] - width, cells.shape[dim], axis=dim)
        cells = jnp.concatenate(
            [
                lax.ppermute(tail, axis, [(i, (i + 1) % count) for i in range(ends)]),
                cells,
                lax.ppermute(head, axis, [((i + 1) % count, i) for i in range(ends)]),
            ],
            axis=dim,
        )
    return cells


def silu_slope(pre_act):
    sigmoid_value = jax.nn.sigmoid(pre_act)
    return sigmoid_value * (1.0 + pre_act * (1.0 - sigmoid_value))


def unfold_taps(padded):
    first_size = padded.shape[1] - 2
    second_size = padded.shape[2] - 2
    third_size = padded.shape[3] - 2
    pieces = [
        padded[:, i : i + first_size, j : j + second_size, k : k + third_size, :]
        for i in range(3)
        for j in range(3)
        for k in range(3)
    ]
    stacked = jnp.concatenate(pieces, axis=-1)
    return stacked.reshape(-1, stacked.shape[-1])


def to_blocks(volume):
    shape = volume.shape
    folded = volume.reshape(
        shape[0], shape[1] // 2, 2, shape[2] // 2, 2, shape[3] // 2, 2, shape[4]
    )
    folded = folded.transpose(0, 1, 3, 5, 2, 4, 6, 7)
    return folded.reshape(-1, 8 * shape[4])


def from_blocks(blocked, shape):
    folded = blocked.reshape(
        shape[0], shape[1] // 2, shape[2] // 2, shape[3] // 2, 2, 2, 2, shape[4]
    )
    folded = folded.transpose(0, 1, 4, 2, 5, 3, 6, 7)
    return folded.reshape(shape)


def flip_taps(w_conv):
    width_in = w_conv.shape[1]
    return (
        w_conv.reshape(27, width_in, width_in)[::-1]
        .transpose(0, 2, 1)
        .reshape(27 * width_in, width_in)
    )


def deep_level(hidden, upstream, w_down, w_up):
    width_in = hidden.shape[-1]
    width_deep = w_down.shape[1]
    hid_blocks = to_blocks(hidden)
    up_blocks = to_blocks(upstream)
    pre_deep = jnp.dot(hid_blocks, w_down, preferred_element_type=jnp.float32)
    deep_act = jax.nn.silu(pre_deep).astype(jnp.bfloat16)
    w_up_back = (
        w_up.reshape(8, width_deep, width_in).transpose(0, 2, 1).reshape(8 * width_in, width_deep)
    )
    grad_act = jnp.dot(up_blocks, w_up_back, preferred_element_type=jnp.float32)
    grad_up = lax.dot_general(
        deep_act, up_blocks, (((0,), (0,)), ((), ())), preferred_element_type=jnp.float32
    )
    grad_up = (
        grad_up.reshape(width_deep, 8, width_in)
        .transpose(1, 0, 2)
        .reshape(8 * width_deep, width_in)
    )
    grad_deep = (grad_act * silu_slope(pre_deep)).astype(jnp.bfloat16)
    grad_down = lax.dot_general(
        hid_blocks, grad_deep, (((0,), (0,)), ((), ())), preferred_element_type=jnp.float32
    )
    back_blocks = jnp.dot(grad_deep, w_down.T, preferred_element_type=jnp.float32).astype(
        jnp.bfloat16
    )
    return (grad_down, grad_up, from_blocks(back_blocks, hidden.shape))


def per_device(inputs, cotangent, w_conv, w_down, w_up):
    width_in = w_conv.shape[1]
    edge_pad = ((0, 0), (0, 0), (1, 1), (1, 1), (0, 0))
    slab_in = extended(inputs, (("sp", 1),), 1)
    columns = unfold_taps(jnp.pad(slab_in, edge_pad))
    pre_conv = jnp.dot(columns, w_conv, preferred_element_type=jnp.float32)
    hidden = jax.nn.silu(pre_conv).astype(jnp.bfloat16).reshape(inputs.shape)
    hidden_crops, upstream_crops = (
        lax.all_to_all(hidden, "sp", split_axis=0, concat_axis=1, tiled=True),
        lax.all_to_all(cotangent, "sp", split_axis=0, concat_axis=1, tiled=True),
    )
    grad_down, grad_up, back_down = deep_level(hidden_crops, upstream_crops, w_down, w_up)
    back_slab = lax.all_to_all(back_down, "sp", split_axis=1, concat_axis=0, tiled=True)
    summed = cotangent.astype(jnp.float32).reshape(-1, width_in) + back_slab.astype(
        jnp.float32
    ).reshape(-1, width_in)
    grad_pre = (summed * silu_slope(pre_conv)).astype(jnp.bfloat16)
    grad_conv = lax.dot_general(
        columns, grad_pre, (((0,), (0,)), ((), ())), preferred_element_type=jnp.float32
    )
    padded_grad = extended(grad_pre.reshape(inputs.shape), (("sp", 1),), 1)
    grad_input = jnp.dot(
        unfold_taps(jnp.pad(padded_grad, edge_pad)),
        flip_taps(w_conv),
        preferred_element_type=jnp.float32,
    )
    grad_input = grad_input.astype(jnp.bfloat16).reshape(inputs.shape)
    local_sums = jnp.concatenate(
        [grad_conv.reshape(-1), grad_down.reshape(-1), grad_up.reshape(-1)]
    )
    within_group = lax.psum(local_sums.astype(jnp.bfloat16), "sp").astype(jnp.float32)
    grad_share = lax.psum_scatter(within_group, "dp", scatter_dimension=0, tiled=True)
    edge_cells = inputs.shape[2]
    crop_total = inputs.shape[0] * lax.axis_size("dp")
    norm_factor = 1.0 / jnp.sqrt(jnp.float32(crop_total * edge_cells * edge_cells * edge_cells))
    return (grad_input, grad_share * norm_factor)


def solution(mesh):
    return jax.shard_map(
        per_device,
        mesh=mesh,
        in_specs=(P("dp", "sp", None, None, None), P("dp", "sp", None, None, None), P(), P(), P()),
        out_specs=(P("dp", "sp", None, None, None), P("dp")),
        check_vma=False,
    )
```

profile of v0, /device:TPU:1, one launch (start us, length us, event | category | flops | bytes accessed | tf_op | source)
XLA Modules:
  0.0 701.0 jit_solution(7751137116307948832)
XLA Ops:
  7.2 0.0 copy-start
  7.2 5.1 collective-permute-start
  12.3 5.1 collective-permute-start.1
  17.4 3.3 all-to-all-start
  20.8 0.0 collective-permute-done
  20.8 0.0 collective-permute-done.1
  20.8 1.3 select_maximum_fusion.2
  22.1 0.0 copy-start.2
  22.1 0.1 slice_dynamic-update-slice_fusion.22
  22.2 0.1 slice_dynamic-update-slice_fusion.21
  22.4 0.1 slice_dynamic-update-slice_fusion.19
  22.5 0.1 slice_dynamic-update-slice_fusion.17
  22.6 0.1 slice_dynamic-update-slice_fusion.16
  22.7 0.1 slice_dynamic-update-slice_fusion.14
  22.8 0.1 slice_dynamic-update-slice_fusion.13
  22.9 0.0 copy-done.5
  22.9 0.1 slice_dynamic-update-slice_fusion.11
  23.1 0.1 slice_dynamic-update-slice_fusion.9
  23.1 0.1 slice_dynamic-update-slice_fusion.8
  23.3 0.1 slice_dynamic-update-slice_fusion.6
  23.3 0.1 slice_dynamic-update-slice_fusion.5
  23.5 0.0 copy-start.4
  23.5 0.1 slice_dynamic-update-slice_fusion.3
  23.6 0.1 slice_dynamic-update-slice_fusion.1
  23.7 0.1 slice_dynamic-update-slice_fusion
  23.8 1.7 copy-done.1
  25.5 1.8 multiply_convert_fusion
  27.3 0.0 all-to-all-done
  27.3 4.6 all-to-all-start.1
  31.9 0.2 copy.21
  32.2 0.1 copy.35
  32.3 0.1 reshape.112
  32.3 5.4 all-to-all-done.1
  37.7 0.1 copy.23
  37.8 0.1 reshape.118
  37.9 0.2 fusion.23
  38.1 0.2 fusion.8
  38.4 0.3 convolution_convert_fusion.4
  38.6 0.0 copy-start.3
  38.7 0.1 reshape.119
  38.7 0.8 copy.24
  39.5 4.2 all-to-all-start.2
  43.7 0.1 reverse_bitcast_fusion
  43.8 1.3 copy.25
  45.1 1.3 dynamic-slice
  47.1 0.3 fusion.7
  47.4 0.4 copy.29
  47.8 0.3 convolution_convert_fusion.1
  48.1 1.4 all-to-all-done.2
  49.6 0.1 fusion.16
  49.7 3.1 fusion
  52.9 3.4 collective-permute-start.2
  56.3 1.9 collective-permute-start.3
  58.2 1.4 pad_maximum_fusion
  59.6 0.0 all-reduce.6.cloned.1.call-update
  59.7 0.0 collective-permute-done.2
  59.7 2.9 collective-permute-done.3
  62.6 0.4 select_maximum_fusion
  62.9 0.1 fusion.22
  63.1 0.6 fusion.21
  64.7 1.7 convolution_convert_fusion.3
  66.5 82.6 %all-reduce.6.cloned.1.call-done = bf16[966656]{0:T(1024)(128)(2,1)} async-done(((bf16[966656]{0:T(1024)(128)(2,1)}), bf16[966656]{0:T(1024)(128)(2,1)}) %all-reduce.6.cloned.1.call-update) | async-done | bytes 1933328 | tf_op jit(solution)/shard_map/psum | solution.py:128
  149.1 543.5 %all-reduce.7 = f32[966656]{0:T(1024)} all-reduce(bf16[966656]{0:T(1024)(128)(2,1)} %all-reduce.6.cloned.1.call-done), channel_id=2, replica_groups=mesh['sp'=8,'dp'=64] {'dp'}, use_global_device_ids=true, to_apply=%region_1.2.clone | all-reduce | flops 966656 | bytes 5799936
  692.6 1.6 dynamic-slice_multiply_fusion
  (46 shorter events, 1.4 us)
Async XLA Ops:
  7.2 30.8 %copy-start = (bf16[1024,256]{1,0:T(8,128)(2,1)S(1)}, bf16[1024,256]{1,0:T(8,128)(2,1)}, u32[]{:S(2)}) copy-start(bf16[1024,256]{1,0:T(8,128)(2,1)} %param.8) | copy-start | bytes 1572868
  7.2 15.7 %copy-start.5 = (bf16[8,1,8,8,128]{4,3,2,1,0:T(8,128)(2,1)S(1)}, bf16[8,1,8,8,128]{4,3,2,1,0:T(8,128)(2,1)}, u32[]{:S(2)}) copy-start(bf16[8,1,8,8,128]{4,3,2,1,0:T(8,128)(2,1)} %param.5) | copy-start | bytes 393220
  7.2 13.6 %collective-permute-start = (bf16[8,1,8,8,128]{4,3,2,1,0:T(8,128)(2,1)}, bf16[8,1,8,8,128]{4,3,2,1,0:T(8,128)(2,1)S(1)}, u32[]{:S(2)}, u32[]{:S(2)}) collective-permute-start(bf16[8,1,8,8,128]{4,3,2,1,0:T(8,128)(2,1)} %param.5), channel_id=1, source_target_pairs={{0,64},{64,128},{128,192},{192,256},{256,320},{320,384},{384,448},... | collective-permute-start | bytes 393224 | tf_op jit(solution)/shard_map/ppermute | solution.py:15
  12.3 8.5 %collective-permute-start.1 = (bf16[8,1,8,8,128]{4,3,2,1,0:T(8,128)(2,1)}, bf16[8,1,8,8,128]{4,3,2,1,0:T(8,128)(2,1)S(1)}, u32[]{:S(2)}, u32[]{:S(2)}) collective-permute-start(bf16[8,1,8,8,128]{4,3,2,1,0:T(8,128)(2,1)} %param.5), channel_id=1, source_target_pairs={{64,0},{128,64},{192,128},{256,192},{320,256},{384,320},{448,384},... | collective-permute-start | bytes 393224 | tf_op jit(solution)/shard_map/ppermute | solution.py:17
  17.4 9.9 %all-to-all-start = ((bf16[8,1,8,8,128]{4,3,2,1,0:T(8,128)(2,1)}), bf16[8,1,8,8,128]{4,3,2,1,0:T(8,128)(2,1)S(1)}, u32[]{:S(2)}, u32[]{:S(2)}) async-start(bf16[8,1,8,8,128]{4,3,2,1,0:T(8,128)(2,1)} %param.6), calls=%async_computation | async-start | bytes 262144 | tf_op jit(solution)/shard_map/all_to_all | solution.py:107
  22.1 3.4 copy-start.2
  23.5 8.4 %copy-start.4 = (bf16[2048,128]{1,0:T(8,128)(2,1)S(1)}, bf16[2048,128]{1,0:T(8,128)(2,1)}, u32[]{:S(2)}) copy-start(bf16[2048,128]{1,0:T(8,128)(2,1)} %param.9) | copy-start | bytes 1572868
  23.8 1.7 copy-start.1
  27.3 10.4 %all-to-all-start.1 = ((bf16[8,1,8,8,128]{4,3,2,1,0:T(8,128)(2,1)}), bf16[8,1,8,8,128]{4,3,2,1,0:T(8,128)(2,1)S(1)}, u32[]{:S(2)}, u32[]{:S(2)}) async-start(bf16[8,1,8,8,128]{4,3,2,1,0:T(8,128)(2,1)} %bitcast.8), calls=%async_computation.1 | async-start | bytes 262144 | tf_op jit(solution)/shard_map/all_to_all | solution.py:106
  38.6 10.9 %copy-start.3 = (bf16[8,1,8,8,128]{4,3,2,1,0:T(8,128)(2,1)S(1)}, bf16[8,1,8,8,128]{4,3,2,1,0:T(8,128)(2,1)}, u32[]{:S(2)}) copy-start(bf16[8,1,8,8,128]{4,3,2,1,0:T(8,128)(2,1)} %param.6) | copy-start | bytes 393220
  39.5 10.1 %all-to-all-start.2 = ((bf16[1,8,8,8,128]{4,3,2,0,1:T(8,128)(2,1)}), bf16[1,8,8,8,128]{4,3,2,0,1:T(8,128)(2,1)S(1)}, u32[]{:S(2)}, u32[]{:S(2)}) async-start(bf16[1,8,8,8,128]{4,3,2,0,1:T(8,128)(2,1)} %bitcast.12), calls=%async_computation.2 | async-start | bytes 262144 | tf_op jit(solution)/shard_map/all_to_all | solution.py:110
  43.7 105.4 %all-reduce.6.cloned.1.call-start = ((), (), s32[]{:S(2)}) async-start(), calls=%async_computation.3 | async-start | bytes 3866624 | tf_op jit(solution)/shard_map/psum | solution.py:128
  52.9 6.8 collective-permute-start.2
  56.3 6.3 collective-permute-start.3
Sparse Core Ops, SparseCore 0:
  59.8 89.2 all-reduce.5
where the time goes:
time: 713 us; the launch traced here: 701 us
  blocking collectives  544 us (76%)
  waiting for transfers between devices  92.4 us (13%)
  starting transfers between devices  27.8 us (4%)
  between operations  15.3 us (2%)
  local copies, waits for them, and re-layouts  9.27 us (1%)
  matrix products  7.98 us (1%)
    unnamed x1, blocking collectives  544 us
    psum x1, waiting for transfers between devices, per_device(): lax.psum(local_sums.astype(jnp.bfloat16), 'sp').astype(jnp.float32)  82.6 us
  transfers between devices with their start and end apart: 8, of which 4 were waited for; matrix products, arithmetic and copies ran while one was open for 2% of the time, Pallas kernels for 0%

commit v1 on v0

v1 whole, which is shorter than its diff:
```python
import math

import jax
import jax.numpy as jnp
from jax import lax
from jax.experimental import pallas as pl
from jax.experimental.pallas import tpu as pltpu
from jax.sharding import PartitionSpec as P

MESH = pl.DeviceIdType.MESH
BF = jnp.bfloat16
F32 = jnp.float32

STARTS = (0, 14, 29, 43)
OFFSETS = (0, 6, 4, 10)
SHARE = 118


def silu_slope(pre_act):
    sigmoid_value = jax.nn.sigmoid(pre_act)
    return sigmoid_value * (1.0 + pre_act * (1.0 - sigmoid_value))


def unfold_taps(volume):
    padded = jnp.pad(volume, ((0, 0), (1, 1), (1, 1), (1, 1), (0, 0)))
    size = volume.shape[1]
    pieces = [
        padded[:, i : i + size, j : j + size, k : k + size, :]
        for i in range(3)
        for j in range(3)
        for k in range(3)
    ]
    stacked = jnp.concatenate(pieces, axis=-1)
    return stacked.reshape(-1, stacked.shape[-1])


def to_blocks(volume):
    shape = volume.shape
    folded = volume.reshape(
        shape[0], shape[1] // 2, 2, shape[2] // 2, 2, shape[3] // 2, 2, shape[4]
    )
    folded = folded.transpose(0, 1, 3, 5, 2, 4, 6, 7)
    return folded.reshape(-1, 8 * shape[4])


def from_blocks(blocked, shape):
    folded = blocked.reshape(
        shape[0], shape[1] // 2, shape[2] // 2, shape[3] // 2, 2, 2, 2, shape[4]
    )
    folded = folded.transpose(0, 1, 4, 2, 5, 3, 6, 7)
    return folded.reshape(shape)


def flip_taps(w_conv):
    width_in = w_conv.shape[1]
    return (
        w_conv.reshape(27, width_in, width_in)[::-1]
        .transpose(0, 2, 1)
        .reshape(27 * width_in, width_in)
    )


def deep_level(hidden, upstream, w_down, w_up):
    width_in = hidden.shape[-1]
    width_deep = w_down.shape[1]
    hid_blocks = to_blocks(hidden)
    up_blocks = to_blocks(upstream)
    pre_deep = jnp.dot(hid_blocks, w_down, preferred_element_type=F32)
    deep_act = jax.nn.silu(pre_deep).astype(BF)
    w_up_back = (
        w_up.reshape(8, width_deep, width_in).transpose(0, 2, 1).reshape(8 * width_in, width_deep)
    )
    grad_act = jnp.dot(up_blocks, w_up_back, preferred_element_type=F32)
    grad_up = lax.dot_general(
        deep_act, up_blocks, (((0,), (0,)), ((), ())), preferred_element_type=F32
    )
    grad_up = (
        grad_up.reshape(width_deep, 8, width_in)
        .transpose(1, 0, 2)
        .reshape(8 * width_deep, width_in)
    )
    grad_deep = (grad_act * silu_slope(pre_deep)).astype(BF)
    grad_down = lax.dot_general(
        hid_blocks, grad_deep, (((0,), (0,)), ((), ())), preferred_element_type=F32
    )
    back_blocks = jnp.dot(grad_deep, w_down.T, preferred_element_type=F32).astype(BF)
    return (grad_down, grad_up, from_blocks(back_blocks, hidden.shape))


def group_wait(ref, sem):
    pltpu.make_async_copy(ref, ref, sem).wait()


def reduce_kernel(
    scale, g_ref, out_ref, pair_in, pair_sum, first_in, first_sum, second_in, second_sum, z_in, final,
    pair_send, pair_recv, first_send, first_recv, second_send, second_recv, z_send, z_recv, out_send, out_recv,
):
    sp = lax.axis_index("sp")
    dp = lax.axis_index("dp")
    core = lax.rem(sp, 2)
    z_lo = lax.div(sp, 2)
    z_hi = lax.div(dp, 16)
    y = lax.rem(lax.div(dp, 4), 4)
    x = lax.rem(dp, 4)
    z = z_hi * 4 + z_lo
    my_first = x + core * (y - x)
    my_second = y + core * (x - y)
    step_first = 1 + 3 * core
    step_second = 4 - 3 * core

    def first_peer(d):
        there = lax.rem(my_first + d, 4)
        return there, {"sp": sp, "dp": dp + (there - my_first) * step_first}

    def second_peer(d):
        there = lax.rem(my_second + d, 4)
        return there, {"sp": sp, "dp": dp + (there - my_second) * step_second}

    barrier = pltpu.get_barrier_semaphore()

    def greet(device):
        pl.semaphore_signal(barrier, inc=1, device_id=device, device_id_type=MESH)

    for d in range(1, 8):
        greet({"sp": lax.rem(sp + d, 8), "dp": dp})
    for d in range(1, 4):
        greet(first_peer(d)[1])
        greet(second_peer(d)[1])
        for t in range(4):
            greet({"sp": 2 * t + core, "dp": y * 4 + x + lax.rem(z_hi + d, 4) * 16})
    pl.semaphore_wait(barrier, 25)

    def send(src, dst, send_sem, recv_sem, device):
        copy = pltpu.make_async_remote_copy(
            src_ref=src, dst_ref=dst, send_sem=send_sem, recv_sem=recv_sem, device_id=device, device_id_type=MESH
        )
        copy.start()

    sibling = {"sp": sp + 1 - 2 * core, "dp": dp}

    def pair_start(q):
        for xx in range(4):
            src = g_ref.at[pl.ds(4 * q, 4), pl.ds(STARTS[xx] + 8 * (1 - core), 8)]
            send(src, pair_in.at[q, :, xx], pair_send.at[q], pair_recv.at[q], sibling)

    def pair_finish(q):
        group_wait(pair_in.at[q], pair_recv.at[q])
        for yy in range(4):
            for xx in range(4):
                own = g_ref[4 * q + yy, pl.ds(STARTS[xx] + 8 * core, 8)].astype(F32)
                total = own + pair_in[q, yy, xx].astype(F32)
                pair_sum[q, xx + core * (yy - xx), yy + core * (xx - yy)] = total.astype(BF)
        for d in range(1, 4):
            there, device = first_peer(d)
            send(pair_sum.at[q, there], first_in.at[q, 3 - d], first_send.at[q], first_recv.at[q], device)

    def first_finish(q):
        group_wait(first_in.at[q], first_recv.at[q])
        for s in range(4):
            total = pair_sum[q, my_first, s].astype(F32)
            for d in range(3):
                total = total + first_in[q, d, s].astype(F32)
            first_sum[q, s] = total.astype(BF)
        for d in range(1, 4):
            there, device = second_peer(d)
            send(first_sum.at[q, there], second_in.at[q, 3 - d], second_send.at[q], second_recv.at[q], device)

    def second_finish(q):
        group_wait(second_in.at[q], second_recv.at[q])
        total = first_sum[q, my_second].astype(F32)
        for d in range(3):
            total = total + second_in[q, d].astype(F32)
        second_sum[q] = total.astype(BF)
        for t in range(4):
            @pl.when(4 * q + t != z)
            def _():
                slot = lax.rem(z - (4 * q + t) + 16, 16) - 1
                send(
                    second_sum.at[q, pl.ds(2 * t, 2)], z_in.at[slot], z_send.at[q, t], z_recv,
                    {"sp": 2 * t + core, "dp": dp + (q - z_hi) * 16},
                )

    order = (3, 2, 1, 0)
    for q in order:
        pair_start(q)
    for q in order:
        pair_finish(q)
    for q in order:
        first_finish(q)
    for q in order:
        second_finish(q)

    group_wait(z_in, z_recv)
    total = second_sum[z_hi, pl.ds(2 * z_lo, 2)].astype(F32)
    for d in range(15):
        total = total + z_in[d].astype(F32)
    place = 4 * core + z_lo
    final[place] = total * scale
    for d in range(1, 8):
        send(final.at[place], final.at[place], out_send, out_recv, {"sp": lax.rem(sp + d, 8), "dp": dp})
    group_wait(final.at[pl.ds(0, 7)], out_recv)
    rows = final[...].reshape(128, 128)
    for xx in range(4):
        @pl.when(x == xx)
        def _():
            out_ref[...] = rows[OFFSETS[xx] : OFFSETS[xx] + SHARE]

    for q in order:
        group_wait(pair_in.at[q], pair_send.at[q])
        group_wait(first_in.at[q], first_send.at[q])
        group_wait(second_in.at[q], second_send.at[q])
        for t in range(4):
            @pl.when(4 * q + t != z)
            def _():
                group_wait(z_in.at[0], z_send.at[q, t])
    group_wait(final.at[pl.ds(0, 7)], out_send)


def reduce_grads(rows, scale):
    def kernel(*refs):
        reduce_kernel(scale, *refs)

    dma = pltpu.SemaphoreType.DMA
    return pl.pallas_call(
        kernel,
        out_shape=jax.ShapeDtypeStruct((SHARE, 128), F32),
        in_specs=[pl.BlockSpec(memory_space=pltpu.VMEM)],
        out_specs=pl.BlockSpec(memory_space=pltpu.VMEM),
        scratch_shapes=[
            pltpu.VMEM((4, 4, 4, 8, 8, 128), BF),
            pltpu.VMEM((4, 4, 4, 8, 8, 128), BF),
            pltpu.VMEM((4, 3, 4, 8, 8, 128), BF),
            pltpu.VMEM((4, 4, 8, 8, 128), BF),
            pltpu.VMEM((4, 3, 8, 8, 128), BF),
            pltpu.VMEM((4, 8, 8, 128), BF),
            pltpu.VMEM((15, 2, 8, 128), BF),
            pltpu.VMEM((8, 2, 8, 128), F32),
            dma((4,)), dma((4,)), dma((4,)), dma((4,)), dma((4,)), dma((4,)), dma((4, 4)), dma, dma, dma,
        ],
        compiler_params=pltpu.CompilerParams(
            collective_id=0, has_side_effects=True, vmem_limit_bytes=32 * 1024 * 1024
        ),
        name="reduce_grads",
    )(rows)


def per_device(inputs, cotangent, w_conv, w_down, w_up):
    width_in = w_conv.shape[1]
    crop = lax.all_to_all(inputs, "sp", split_axis=0, concat_axis=1, tiled=True)
    upstream = lax.all_to_all(cotangent, "sp", split_axis=0, concat_axis=1, tiled=True)
    columns = unfold_taps(crop)
    pre_conv = jnp.dot(columns, w_conv, preferred_element_type=F32)
    hidden = jax.nn.silu(pre_conv).astype(BF).reshape(crop.shape)
    grad_down, grad_up, back_down = deep_level(hidden, upstream, w_down, w_up)
    summed = upstream.astype(F32).reshape(-1, width_in) + back_down.astype(F32).reshape(-1, width_in)
    grad_pre = (summed * silu_slope(pre_conv)).astype(BF)
    grad_conv = lax.dot_general(
        columns, grad_pre, (((0,), (0,)), ((), ())), preferred_element_type=F32
    )
    grad_input = jnp.dot(
        unfold_taps(grad_pre.reshape(crop.shape)), flip_taps(w_conv), preferred_element_type=F32
    )
    grad_input = grad_input.astype(BF).reshape(crop.shape)
    grad_input = lax.all_to_all(grad_input, "sp", split_axis=1, concat_axis=0, tiled=True)
    rows = jnp.concatenate(
        [grad_conv.astype(BF), grad_down.astype(BF).reshape(-1, 128), grad_up.astype(BF)], axis=0
    ).reshape(16, 59, 8, 128)
    edge = inputs.shape[2]
    crops = inputs.shape[0] * lax.axis_size("dp")
    share = reduce_grads(rows, 1.0 / math.sqrt(crops * edge * edge * edge))
    return (grad_input, share.reshape(-1))


def solution(mesh):
    return jax.shard_map(
        per_device,
        mesh=mesh,
        in_specs=(P("dp", "sp", None, None, None), P("dp", "sp", None, None, None), P(), P(), P()),
        out_specs=(P("dp", "sp", None, None, None), P("dp")),
        check_vma=False,
    )
```

time: 713 us -> 92.6 us (0.13); the launches traced: 701 us -> 91.8 us
  blocking collectives: 544 us -> 0 us
  waiting for transfers between devices: 92.4 us -> 2.71 us
  Pallas kernels: 0 us -> 36.6 us
  local copies, waits for them, and re-layouts: 9.27 us -> 24.8 us
  between operations: 15.3 us -> 1.34 us
  starting transfers between devices: 27.8 us -> 18.8 us
    unnamed x1 -> x0, blocking collectives: 544 us -> none
    psum x1 -> x0, waiting for transfers between devices: 82.6 us -> none  [per_device(): lax.psum(local_sums.astype(jnp.bfloat16), 'sp').astype(jnp.float32)]
    pallas_call x0 -> x1, Pallas kernels: none -> 36.6 us  [reduce_grads(): pl.pallas_call(kernel, out_shape=jax.ShapeDtypeStruct((SHARE, 128), F32),...]
    ppermute x4 -> x0, starting transfers between devices: 15.5 us -> none  [the longest x2 8.47 us: extended(): lax.ppermute(tail, axis, [(i, (i + 1) % count) for i in range(ends)])]
    unnamed x66 -> x82, local copies, waits for them, and re-layouts: 5.76 us -> 16.7 us
  transfers between devices with their start and end apart: 8 -> 3, of which waited for: 4 -> 2; matrix products, arithmetic and copies ran while one was open for 2% -> 8% of each run, Pallas kernels for 0% -> 40%
where the time goes in v1:
time: 92.6 us; the launch traced here: 91.8 us
  Pallas kernels  36.6 us (40%)
  local copies, waits for them, and re-layouts  24.8 us (27%)
  starting transfers between devices  18.8 us (20%)
  matrix products  7.33 us (8%)
  waiting for transfers between devices  2.71 us (3%)
  between operations  1.34 us (1%)
    pallas_call x1, Pallas kernels, reduce_grads(): pl.pallas_call(kernel, out_shape=jax.ShapeDtypeStruct((SHARE, 128), F32),...  36.6 us
    unnamed x82, local copies, waits for them, and re-layouts  16.7 us
    all_to_all x1, starting transfers between devices, per_device(): crop = lax.all_to_all(inputs, 'sp', split_axis=0, concat_axis=1, tiled=True)  10.3 us
    all_to_all x1, starting transfers between devices, per_device(): lax.all_to_all(cotangent, 'sp', split_axis=0, concat_axis=1, tiled=True)  4.25 us
    all_to_all x1, starting transfers between devices, per_device(): lax.all_to_all(grad_input, 'sp', split_axis=1, concat_axis=0, tiled=True)  4.25 us
    dot_general x1, matrix products, per_device(): lax.dot_general(columns, grad_pre, (((0,), (0,)), ((), ())), preferred_el...  3.14 us
    slice x4, local copies, waits for them, and re-layouts, unfold_taps(): padded[:, i:i + size, j:j + size, k:k + size, :]  3.1 us
    transpose x2, local copies, waits for them, and re-layouts, flip_taps(): return w_conv.reshape(27, width_in, width_in)[::-1].transpose(0, 2, 1).re...  2.88 us
  transfers between devices with their start and end apart: 3, of which 2 were waited for; matrix products, arithmetic and copies ran while one was open for 8% of the time, Pallas kernels for 40%

profile of v1, /device:TPU:1, one launch (start us, length us, event | category | flops | bytes accessed | tf_op | source)
XLA Modules:
  0.0 91.8 jit_solution(704702041437827682)
XLA Ops:
  0.6 0.0 copy-start
  0.6 10.3 %all-to-all-start.1 = ((bf16[8,1,8,8,128]{4,3,2,1,0:T(8,128)(2,1)}), bf16[8,1,8,8,128]{4,3,2,1,0:T(8,128)(2,1)S(1)}, u32[]{:S(2)}, u32[]{:S(2)}) async-start(bf16[8,1,8,8,128]{4,3,2,1,0:T(8,128)(2,1)} %param.5), calls=%async_computation.1 | async-start | bytes 262144 | tf_op jit(solution)/shard_map/all_to_all | solution.py:249
  10.9 1.2 %copy.19 = bf16[8,128,256]{2,1,0:T(8,128)(2,1)S(1)} copy(bf16[8,128,256]{1,2,0:T(8,128)(2,1)} %bitcast.163) | data formatting | bytes 1048576 | tf_op jit(solution)/shard_map/transpose | solution.py:71
  12.2 1.2 %reverse_bitcast_fusion = bf16[27,128,128]{1,2,0:T(8,128)(2,1)S(1)} fusion(bf16[27,128,128]{2,1,0:T(8,128)(2,1)} %bitcast.123), kind=kLoop, calls=%fused_computation.61 | loop fusion | bytes 1769472 | tf_op jit(solution)/shard_map/transpose | solution.py:58
  13.4 1.7 %copy.22 = bf16[27,128,128]{2,1,0:T(8,128)(2,1)} copy(bf16[27,128,128]{1,2,0:T(8,128)(2,1)S(1)} %reverse_bitcast_fusion) | data formatting | bytes 1769472 | tf_op jit(solution)/shard_map/transpose | solution.py:58
  15.1 1.7 %all-to-all-done.1 = bf16[8,1,8,8,128]{4,3,2,1,0:T(8,128)(2,1)S(1)} async-done(((bf16[8,1,8,8,128]{4,3,2,1,0:T(8,128)(2,1)}), bf16[8,1,8,8,128]{4,3,2,1,0:T(8,128)(2,1)S(1)}, u32[]{:S(2)}, u32[]{:S(2)}) %all-to-all-start.1) | async-done | bytes 131104 | tf_op jit(solution)/shard_map/all_to_all | solution.py:249
  16.8 4.3 %all-to-all-start = ((bf16[8,1,8,8,128]{4,3,2,1,0:T(8,128)(2,1)}), bf16[8,1,8,8,128]{4,3,2,1,0:T(8,128)(2,1)S(1)}, u32[]{:S(2)}, u32[]{:S(2)}) async-start(bf16[8,1,8,8,128]{4,3,2,1,0:T(8,128)(2,1)} %param.6), calls=%async_computation | async-start | bytes 262144 | tf_op jit(solution)/shard_map/all_to_all | solution.py:250
  21.0 0.5 pad_slice_fusion.26
  21.5 0.2 pad_slice_fusion.27
  21.7 0.0 copy-start.2
  22.8 0.0 copy-start.1
  22.8 1.7 %copy-done.1 = bf16[512,3456]{1,0:T(8,128)(2,1)} copy-done((bf16[512,3456]{1,0:T(8,128)(2,1)}, bf16[512,3456]{1,0:T(8,128)(2,1)S(1)}, u32[]{:S(2)}) %copy-start.1) | copy-done | bytes 3538968
  24.6 0.0 copy-done.2
  24.6 1.1 %multiply_convert_fusion = (bf16[512,128]{1,0:T(8,128)(2,1)S(1)}, f32[512,128]{1,0:T(8,128)S(1)}) fusion(bf16[512,3456]{1,0:T(8,128)(2,1)S(1)} %constant_dynamic-update-slice_fusion, bf16[3456,128]{1,0:T(8,128)(2,1)S(1)} %copy-done.2), kind=kOutput, calls=%fused_computation.65 | convolution fusion | flops 453312512 | bytes 4816896 | tf_op jit(solution)/shard_map/dot_general | solution.py:252
  25.7 0.1 copy.33
  25.8 0.1 reshape.134
  25.9 1.0 %all-to-all-done = bf16[8,1,8,8,128]{4,3,2,1,0:T(8,128)(2,1)S(1)} async-done(((bf16[8,1,8,8,128]{4,3,2,1,0:T(8,128)(2,1)}), bf16[8,1,8,8,128]{4,3,2,1,0:T(8,128)(2,1)S(1)}, u32[]{:S(2)}, u32[]{:S(2)}) %all-to-all-start) | async-done | bytes 131104 | tf_op jit(solution)/shard_map/all_to_all | solution.py:250
  26.9 0.1 copy.34
  27.0 0.1 reshape.131
  27.1 0.2 fusion.8
  27.3 0.2 fusion.1
  27.5 0.3 fusion
  27.8 0.3 convolution_convert_fusion.2
  28.1 0.3 convolution_convert_fusion.1
  28.4 0.2 reshape.144
  28.7 0.1 copy.21
  28.8 0.1 fusion.3
  28.9 3.1 %convolution_convert_fusion = bf16[3456,128]{1,0:T(8,128)(2,1)S(1)} fusion(bf16[512,3456]{1,0:T(8,128)(2,1)} %copy-done.1, bf16[512,128]{1,0:T(8,128)(2,1)S(1)} %fusion.3), kind=kOutput, calls=%fused_computation | convolution fusion | flops 453427200 | bytes 4554752 | tf_op jit(solution)/shard_map/dot_general | solution.py:257
  32.0 1.0 %pad_slice_fusion.1 = (bf16[1,8,8,8,128]{4,3,2,1,0:T(8,128)(2,1)}, bf16[1,8,8,8,128]{4,3,2,1,0:T(8,128)(2,1)}, bf16[1,8,8,8,128]{4,3,2,1,0:T(8,128)(2,1)}, bf16[...) fusion(bf16[1,8,8,8,128]{4,3,2,1,0:T(8,128)(2,1)S(1)} %bitcast.115), kind=kLoop, calls=%fused_computation.2 | loop fusion | bytes 1048576 | tf_op jit(solution)/shard_map/slice | solution.py:28
  33.0 1.5 %pad_slice_fusion = (bf16[1,8,8,8,128]{4,3,2,1,0:T(8,128)(2,1)S(1)}, bf16[1,8,8,8,128]{4,3,2,1,0:T(8,128)(2,1)}, bf16[1,8,8,8,128]{4,3,2,1,0:T(8,128)(2,1)}, bf1...) fusion(bf16[1,8,8,8,128]{4,3,2,1,0:T(8,128)(2,1)S(1)} %bitcast.116), kind=kLoop, calls=%fused_computation.1 | loop fusion | bytes 2621440 | tf_op jit(solution)/shard_map/slice | solution.py:28
  34.5 0.2 reshape.139
  34.7 0.0 copy-start.7
  34.7 0.0 copy-start.6
  34.7 0.0 copy-start.5
  34.7 0.0 copy-start.4
  34.7 0.0 copy-start.13
  34.7 0.0 copy-start.12
  34.7 0.0 copy-start.11
  34.7 0.0 copy-start.10
  34.7 0.0 copy-start.9
  34.7 0.0 copy-start.8
  34.8 1.1 %constant_dynamic-update-slice_fusion.53 = bf16[512,3456]{1,0:T(8,128)(2,1)S(1)} fusion(bf16[512,128]{1,0:T(8,128)(2,1)} %bitcast.180), kind=kLoop, calls=%fused_computation.124 | loop fusion | bytes 262144
  35.8 0.9 %constant_dynamic-update-slice_fusion.52 = bf16[512,3456]{1,0:T(8,128)(2,1)S(1)} fusion(bf16[512,3456]{1,0:T(8,128)(2,1)S(1)} %constant_dynamic-update-slice_fusion.53, bf16[512,128]{1,0:T(8,128)(2,1)} %bitcast.162), kind=kLoop, calls=%fused_computation.123 | loop fusion | bytes 262144
  36.8 0.9 %constant_dynamic-update-slice_fusion.51 = bf16[512,3456]{1,0:T(8,128)(2,1)S(1)} fusion(bf16[512,3456]{1,0:T(8,128)(2,1)S(1)} %constant_dynamic-update-slice_fusion.52, bf16[512,128]{1,0:T(8,128)(2,1)} %bitcast.161), kind=kLoop, calls=%fused_computation.122 | loop fusion | bytes 262144
  37.7 0.9 %constant_dynamic-update-slice_fusion.50 = bf16[512,3456]{1,0:T(8,128)(2,1)S(1)} fusion(bf16[512,3456]{1,0:T(8,128)(2,1)S(1)} %constant_dynamic-update-slice_fusion.51, bf16[512,128]{1,0:T(8,128)(2,1)} %bitcast.160), kind=kLoop, calls=%fused_computation.121 | loop fusion | bytes 262144
  38.7 0.9 %constant_dynamic-update-slice_fusion.49 = bf16[512,3456]{1,0:T(8,128)(2,1)S(1)} fusion(bf16[512,3456]{1,0:T(8,128)(2,1)S(1)} %constant_dynamic-update-slice_fusion.50, bf16[512,128]{1,0:T(8,128)(2,1)} %bitcast.159), kind=kLoop, calls=%fused_computation.120 | loop fusion | bytes 262144
  39.6 0.9 %constant_dynamic-update-slice_fusion.48 = bf16[512,3456]{1,0:T(8,128)(2,1)S(1)} fusion(bf16[512,3456]{1,0:T(8,128)(2,1)S(1)} %constant_dynamic-update-slice_fusion.49, bf16[512,128]{1,0:T(8,128)(2,1)} %bitcast.157), kind=kLoop, calls=%fused_computation.119 | loop fusion | bytes 262144
  40.5 0.9 %constant_dynamic-update-slice_fusion.47 = bf16[512,3456]{1,0:T(8,128)(2,1)S(1)} fusion(bf16[512,3456]{1,0:T(8,128)(2,1)S(1)} %constant_dynamic-update-slice_fusion.48, bf16[512,128]{1,0:T(8,128)(2,1)} %bitcast.155), kind=kLoop, calls=%fused_computation.118 | loop fusion | bytes 262144
  41.5 0.9 %constant_dynamic-update-slice_fusion.46 = bf16[512,3456]{1,0:T(8,128)(2,1)S(1)} fusion(bf16[512,3456]{1,0:T(8,128)(2,1)S(1)} %constant_dynamic-update-slice_fusion.47, bf16[512,128]{1,0:T(8,128)(2,1)} %bitcast.153), kind=kLoop, calls=%fused_computation.117 | loop fusion | bytes 262144
  42.4 0.9 %constant_dynamic-update-slice_fusion.45 = bf16[512,3456]{1,0:T(8,128)(2,1)S(1)} fusion(bf16[512,3456]{1,0:T(8,128)(2,1)S(1)} %constant_dynamic-update-slice_fusion.46, bf16[512,128]{1,0:T(8,128)(2,1)} %bitcast.151), kind=kLoop, calls=%fused_computation.116 | loop fusion | bytes 262144
  43.4 0.9 %constant_dynamic-update-slice_fusion.44 = bf16[512,3456]{1,0:T(8,128)(2,1)S(1)} fusion(bf16[512,3456]{1,0:T(8,128)(2,1)S(1)} %constant_dynamic-update-slice_fusion.45, bf16[512,128]{1,0:T(8,128)(2,1)} %bitcast.149), kind=kLoop, calls=%fused_computation.115 | loop fusion | bytes 262144
  44.3 0.9 %constant_dynamic-update-slice_fusion.43 = bf16[512,3456]{1,0:T(8,128)(2,1)S(1)} fusion(bf16[512,3456]{1,0:T(8,128)(2,1)S(1)} %constant_dynamic-update-slice_fusion.44, bf16[512,128]{1,0:T(8,128)(2,1)} %bitcast.147), kind=kLoop, calls=%fused_computation.114 | loop fusion | bytes 262144
  45.2 0.9 %constant_dynamic-update-slice_fusion.42 = bf16[512,3456]{1,0:T(8,128)(2,1)S(1)} fusion(bf16[512,3456]{1,0:T(8,128)(2,1)S(1)} %constant_dynamic-update-slice_fusion.43, bf16[512,128]{1,0:T(8,128)(2,1)} %bitcast.145), kind=kLoop, calls=%fused_computation.113 | loop fusion | bytes 262144
  46.2 0.9 %constant_dynamic-update-slice_fusion.41 = bf16[512,3456]{1,0:T(8,128)(2,1)S(1)} fusion(bf16[512,3456]{1,0:T(8,128)(2,1)S(1)} %constant_dynamic-update-slice_fusion.42, bf16[512,128]{1,0:T(8,128)(2,1)} %bitcast.143), kind=kLoop, calls=%fused_computation.112 | loop fusion | bytes 262144
  47.2 0.0 copy-done.6
  47.5 0.0 copy-done.13
  47.6 0.0 copy-done.10
  47.8 1.7 %convolution_convert_fusion.3 = bf16[512,128]{1,0:T(8,128)(2,1)} fusion(bf16[512,3456]{1,0:T(8,128)(2,1)S(1)} %constant_dynamic-update-slice_fusion.27, bf16[3456,128]{1,0:T(8,128)(2,1)S(1)} %bitcast.124), kind=kOutput, calls=%fused_computation.56 | convolution fusion | flops 453050368 | bytes 4554752 | tf_op jit(solution)/shard_map/dot_general | solution.py:260
  49.6 4.3 %all-to-all-start.2 = ((bf16[1,8,8,8,128]{4,3,2,0,1:T(8,128)(2,1)}), bf16[1,8,8,8,128]{4,3,2,0,1:T(8,128)(2,1)S(1)}, u32[]{:S(2)}, u32[]{:S(2)}) async-start(bf16[1,8,8,8,128]{4,3,2,0,1:T(8,128)(2,1)} %bitcast.69), calls=%async_computation.2 | async-start | bytes 262144 | tf_op jit(solution)/shard_map/all_to_all | solution.py:264
  53.8 0.1 pad_maximum_fusion
  53.9 36.6 %reduce_grads.1 = f32[118,128]{1,0:T(8,128)S(1)} custom-call(bf16[16,59,8,128]{3,2,1,0:T(8,128)(2,1)S(1)} %bitcast.113), custom_call_target="tpu_custom_call" | custom-call | tf_op jit(solution)/shard_map/reduce_grads/pallas_call | solution.py:224
  90.5 0.0 all-to-all-done.2
  90.5 0.7 copy.89
  91.2 0.6 copy.90
  (51 shorter events, 1.4 us)
Async XLA Ops:
  0.6 26.4 %copy-start = (bf16[1024,256]{1,0:T(8,128)(2,1)S(1)}, bf16[1024,256]{1,0:T(8,128)(2,1)}, u32[]{:S(2)}) copy-start(bf16[1024,256]{1,0:T(8,128)(2,1)} %param.8) | copy-start | bytes 1572868
  0.6 16.1 %all-to-all-start.1 = ((bf16[8,1,8,8,128]{4,3,2,1,0:T(8,128)(2,1)}), bf16[8,1,8,8,128]{4,3,2,1,0:T(8,128)(2,1)S(1)}, u32[]{:S(2)}, u32[]{:S(2)}) async-start(bf16[8,1,8,8,128]{4,3,2,1,0:T(8,128)(2,1)} %param.5), calls=%async_computation.1 | async-start | bytes 262144 | tf_op jit(solution)/shard_map/all_to_all | solution.py:249
  16.8 10.1 %all-to-all-start = ((bf16[8,1,8,8,128]{4,3,2,1,0:T(8,128)(2,1)}), bf16[8,1,8,8,128]{4,3,2,1,0:T(8,128)(2,1)S(1)}, u32[]{:S(2)}, u32[]{:S(2)}) async-start(bf16[8,1,8,8,128]{4,3,2,1,0:T(8,128)(2,1)} %param.6), calls=%async_computation | async-start | bytes 262144 | tf_op jit(solution)/shard_map/all_to_all | solution.py:250
  21.7 2.9 %copy-start.2 = (bf16[3456,128]{1,0:T(8,128)(2,1)S(1)}, bf16[3456,128]{1,0:T(8,128)(2,1)}, u32[]{:S(2)}) copy-start(bf16[3456,128]{1,0:T(8,128)(2,1)} %param.7) | copy-start | bytes 2654212
  22.8 1.8 %copy-start.1 = (bf16[512,3456]{1,0:T(8,128)(2,1)}, bf16[512,3456]{1,0:T(8,128)(2,1)S(1)}, u32[]{:S(2)}) copy-start(bf16[512,3456]{1,0:T(8,128)(2,1)S(1)} %constant_dynamic-update-slice_fusion) | copy-start | bytes 10616836
  34.7 12.5 %copy-start.7 = (bf16[1,8,8,8,128]{4,3,2,1,0:T(8,128)(2,1)S(1)}, bf16[1,8,8,8,128]{4,3,2,1,0:T(8,128)(2,1)}, u32[]{:S(2)}) copy-start(bf16[1,8,8,8,128]{4,3,2,1,0:T(8,128)(2,1)} %get-tuple-element.17) | copy-start | bytes 393220
  34.7 12.6 %copy-start.6 = (bf16[1,8,8,8,128]{4,3,2,1,0:T(8,128)(2,1)S(1)}, bf16[1,8,8,8,128]{4,3,2,1,0:T(8,128)(2,1)}, u32[]{:S(2)}) copy-start(bf16[1,8,8,8,128]{4,3,2,1,0:T(8,128)(2,1)} %get-tuple-element.18) | copy-start | bytes 393220
  34.7 12.6 %copy-start.5 = (bf16[1,8,8,8,128]{4,3,2,1,0:T(8,128)(2,1)S(1)}, bf16[1,8,8,8,128]{4,3,2,1,0:T(8,128)(2,1)}, u32[]{:S(2)}) copy-start(bf16[1,8,8,8,128]{4,3,2,1,0:T(8,128)(2,1)} %get-tuple-element.19) | copy-start | bytes 393220
  34.7 12.6 %copy-start.4 = (bf16[1,8,8,8,128]{4,3,2,1,0:T(8,128)(2,1)S(1)}, bf16[1,8,8,8,128]{4,3,2,1,0:T(8,128)(2,1)}, u32[]{:S(2)}) copy-start(bf16[1,8,8,8,128]{4,3,2,1,0:T(8,128)(2,1)} %get-tuple-element.20) | copy-start | bytes 393220
  34.7 12.8 %copy-start.13 = (bf16[1,8,8,8,128]{4,3,2,1,0:T(8,128)(2,1)S(1)}, bf16[1,8,8,8,128]{4,3,2,1,0:T(8,128)(2,1)}, u32[]{:S(2)}) copy-start(bf16[1,8,8,8,128]{4,3,2,1,0:T(8,128)(2,1)} %get-tuple-element.24) | copy-start | bytes 393220
  34.7 12.8 %copy-start.12 = (bf16[1,8,8,8,128]{4,3,2,1,0:T(8,128)(2,1)S(1)}, bf16[1,8,8,8,128]{4,3,2,1,0:T(8,128)(2,1)}, u32[]{:S(2)}) copy-start(bf16[1,8,8,8,128]{4,3,2,1,0:T(8,128)(2,1)} %get-tuple-element.25) | copy-start | bytes 393220
  34.7 12.8 %copy-start.11 = (bf16[1,8,8,8,128]{4,3,2,1,0:T(8,128)(2,1)S(1)}, bf16[1,8,8,8,128]{4,3,2,1,0:T(8,128)(2,1)}, u32[]{:S(2)}) copy-start(bf16[1,8,8,8,128]{4,3,2,1,0:T(8,128)(2,1)} %get-tuple-element.26) | copy-start | bytes 393220
  34.7 12.9 %copy-start.10 = (bf16[1,8,8,8,128]{4,3,2,1,0:T(8,128)(2,1)S(1)}, bf16[1,8,8,8,128]{4,3,2,1,0:T(8,128)(2,1)}, u32[]{:S(2)}) copy-start(bf16[1,8,8,8,128]{4,3,2,1,0:T(8,128)(2,1)} %get-tuple-element.27) | copy-start | bytes 393220
  34.7 12.9 %copy-start.9 = (bf16[1,8,8,8,128]{4,3,2,1,0:T(8,128)(2,1)S(1)}, bf16[1,8,8,8,128]{4,3,2,1,0:T(8,128)(2,1)}, u32[]{:S(2)}) copy-start(bf16[1,8,8,8,128]{4,3,2,1,0:T(8,128)(2,1)} %get-tuple-element.28) | copy-start | bytes 393220
  34.7 13.0 %copy-start.8 = (bf16[1,8,8,8,128]{4,3,2,1,0:T(8,128)(2,1)S(1)}, bf16[1,8,8,8,128]{4,3,2,1,0:T(8,128)(2,1)}, u32[]{:S(2)}) copy-start(bf16[1,8,8,8,128]{4,3,2,1,0:T(8,128)(2,1)} %get-tuple-element.23) | copy-start | bytes 393220
  34.8 13.1 %copy-start.3 = (bf16[27,128,128]{2,1,0:T(8,128)(2,1)S(1)}, bf16[27,128,128]{2,1,0:T(8,128)(2,1)}, u32[]{:S(2)}) copy-start(bf16[27,128,128]{2,1,0:T(8,128)(2,1)} %copy.22) | copy-start | bytes 2654212
  49.6 40.9 %all-to-all-start.2 = ((bf16[1,8,8,8,128]{4,3,2,0,1:T(8,128)(2,1)}), bf16[1,8,8,8,128]{4,3,2,0,1:T(8,128)(2,1)S(1)}, u32[]{:S(2)}, u32[]{:S(2)}) async-start(bf16[1,8,8,8,128]{4,3,2,0,1:T(8,128)(2,1)} %bitcast.69), calls=%async_computation.2 | async-start | bytes 262144 | tf_op jit(solution)/shard_map/all_to_all | solution.py:264

commit v2 on v1

v2 whole, which is shorter than its diff:
```python
import math

import jax
import jax.numpy as jnp
from jax import lax
from jax.experimental import pallas as pl
from jax.experimental.pallas import tpu as pltpu
from jax.sharding import PartitionSpec as P

MESH = pl.DeviceIdType.MESH
BF = jnp.bfloat16
F32 = jnp.float32

STARTS = (0, 14, 29, 43)
OFFSETS = (0, 6, 4, 10)
SHARE = 118
TILES = 59
DOWN_TILE = 3456 // 8
UP_TILE = 5504 // 8


def dot(a, b):
    return jnp.dot(a, b, preferred_element_type=F32)


def dot_first(a, b):
    return lax.dot_general(a, b, (((0,), (0,)), ((), ())), preferred_element_type=F32)


def dot_last(a, b):
    return lax.dot_general(a, b, (((1,), (1,)), ((), ())), preferred_element_type=F32)


def order_matrices(order_ref, back_ref, twice_ref):
    row = lax.broadcasted_iota(jnp.int32, (128, 128), 0)
    column = lax.broadcasted_iota(jnp.int32, (128, 128), 1)

    def source(r):
        tap, b, c = r >> 4, (r >> 2) & 3, r & 3
        return ((tap >> 2) << 6) + ((2 * b + ((tap >> 1) & 1)) << 3) + 2 * c + (tap & 1)

    order_ref[...] = jnp.where(column == source(row), 1.0, 0.0).astype(BF)
    back_ref[...] = jnp.where(row == source(column), 1.0, 0.0).astype(BF)
    channel = lax.broadcasted_iota(jnp.int32, (128, 256), 0)
    place = lax.broadcasted_iota(jnp.int32, (128, 256), 1)
    twice_ref[...] = jnp.where(channel == (place >> 1), 1.0, 0.0).astype(BF)


def flip_weights(w_conv_ref, w_flip_ref):
    for t in range(27):
        block = w_conv_ref[128 * (26 - t) : 128 * (27 - t), :]
        w_flip_ref[128 * t : 128 * (t + 1), :] = block.astype(F32).T.astype(BF)


def fill_columns(columns_ref, volume):
    lines = volume.reshape(64, 8, 128)
    k_at = lax.broadcasted_iota(jnp.int32, (64, 8, 128), 1)
    zero_line = jnp.zeros((8, 1, 8, 128), F32)
    for k in range(3):
        moved = lines
        if k == 0:
            moved = jnp.where(k_at == 0, 0.0, pltpu.roll(lines, 1, axis=1))
        if k == 2:
            moved = jnp.where(k_at == 7, 0.0, pltpu.roll(lines, 7, axis=1))
        planes = moved.reshape(8, 8, 8, 128)
        for j in range(3):
            shifted = planes
            if j == 0:
                shifted = jnp.concatenate([zero_line, planes[:, :7]], axis=1)
            if j == 2:
                shifted = jnp.concatenate([planes[:, 1:], zero_line], axis=1)
            lane = 128 * (3 * j + k)
            columns_ref[64:576, lane : lane + 128] = shifted.reshape(512, 128).astype(BF)


def convolve(columns_ref, weights_ref):
    total = dot(columns_ref[0:512, :], weights_ref[0:1152, :])
    total += dot(columns_ref[64:576, :], weights_ref[1152:2304, :])
    total += dot(columns_ref[128:640, :], weights_ref[2304:3456, :])
    return total


def to_blocks(order, volume):
    side_by_side = jnp.concatenate([volume[128 * a : 128 * (a + 1)] for a in range(4)], axis=1)
    moved = dot(order, side_by_side).astype(BF)
    return [
        jnp.concatenate(
            [moved[16 * t : 16 * (t + 1), 128 * a : 128 * (a + 1)] for a in range(4)], axis=0
        )
        for t in range(8)
    ]


def from_blocks(back, blocks):
    stacked = jnp.concatenate(
        [
            jnp.concatenate(
                [blocks[16 * a : 16 * (a + 1), 128 * t : 128 * (t + 1)] for a in range(4)], axis=1
            )
            for t in range(8)
        ],
        axis=0,
    )
    moved = dot(back, stacked)
    return jnp.concatenate([moved[:, 128 * a : 128 * (a + 1)] for a in range(4)], axis=0)


def put_rows(rows_ref, tile, values):
    count = values.shape[0] // 8
    values = values.reshape(count, 8, 128).astype(BF)
    done = 0
    while done < count:
        block, place = divmod(tile + done, TILES)
        size = min(count - done, TILES - place)
        rows_ref[block, place : place + size] = values[done : done + size]
        done += size


def logistic_parts(pre):
    s = jax.nn.sigmoid(pre)
    return pre * s, s * (1.0 + pre * (1.0 - s))


def forward(crop_ref, w_conv_ref, columns_ref, slope_ref):
    fill_columns(columns_ref, crop_ref[...].reshape(512, 128).astype(F32))
    hidden, slope = logistic_parts(convolve(columns_ref, w_conv_ref))
    slope_ref[...] = slope
    return hidden.astype(BF)


def deep_forward(hid_taps, w_down_ref):
    pre_deep = dot(jnp.concatenate(hid_taps, axis=1), w_down_ref[...])
    act, slope = logistic_parts(pre_deep)
    return act.astype(BF), slope


def up_grads(rows_ref, deep_act, up_taps):
    for t in range(8):
        put_rows(rows_ref, UP_TILE + 32 * t, dot_first(deep_act, up_taps[t]))


def deep_grads(up_taps, slope, w_up_ref):
    grad_act = dot_last(up_taps[0], w_up_ref[0:256, :])
    for t in range(1, 8):
        grad_act += dot_last(up_taps[t], w_up_ref[256 * t : 256 * (t + 1), :])
    return (grad_act * slope).astype(BF)


def down_grads(rows_ref, hid_taps, twice, grad_deep):
    odd = (lax.broadcasted_iota(jnp.int32, (256, 128), 0) & 1) == 1
    doubled = dot(jnp.concatenate(hid_taps, axis=0), twice).astype(BF)
    for t in range(8):
        both = dot_first(doubled[64 * t : 64 * (t + 1)], grad_deep)
        put_rows(rows_ref, DOWN_TILE + 32 * t, jnp.where(odd, both[:, 128:], both[:, :128]))


def pre_grads(cotangent_ref, grad_deep, w_down_ref, back, slope_ref):
    blocks = dot_last(grad_deep, w_down_ref[...]).astype(BF)
    summed = cotangent_ref[...].reshape(512, 128).astype(F32) + from_blocks(back, blocks)
    return summed * slope_ref[...]


def conv_grads_late(rows_ref, turned_ref, padded_ref, grad_pre):
    padded_ref[64:576, 0:128] = grad_pre
    padded_ref[128:640, 128:256] = grad_pre
    total = dot(turned_ref[...], padded_ref[...])
    for i in (1, 2):
        put_rows(rows_ref, 144 * i, total[:, 128 * (i - 1) : 128 * i])


def conv_grads_early(rows_ref, turned_ref, grad_pre):
    put_rows(rows_ref, 0, dot(turned_ref[:, 0:512], grad_pre))


def group_wait(ref, sem):
    pltpu.make_async_copy(ref, ref, sem).wait()


def step_kernel(
    scale,
    inputs_ref, cotangent_ref, w_conv_any, w_down_any, w_up_any,
    grad_input_ref, share_ref,
    crop, upstream, w_conv, w_down, w_up, w_flip, columns, turned, padded, slope, order, back, twice, rows, grad_out,
    pair_in, pair_sum, first_in, first_sum, second_in, second_sum, z_in, final,
    load_sem, own_sem, crop_send, crop_recv, up_send, up_recv, grad_send, grad_recv,
    pair_send, pair_recv, first_send, first_recv, second_send, second_recv, z_send, z_recv, out_send, out_recv,
):
    sp = lax.axis_index("sp")
    dp = lax.axis_index("dp")
    core = lax.rem(sp, 2)
    z_lo = lax.div(sp, 2)
    z_hi = lax.div(dp, 16)
    y = lax.rem(lax.div(dp, 4), 4)
    x = lax.rem(dp, 4)
    z = z_hi * 4 + z_lo
    my_first = x + core * (y - x)
    my_second = y + core * (x - y)
    step_first = 1 + 3 * core
    step_second = 4 - 3 * core

    def member(d):
        there = lax.rem(sp + d, 8)
        return there, {"sp": there, "dp": dp}

    def first_peer(d):
        there = lax.rem(my_first + d, 4)
        return there, {"sp": sp, "dp": dp + (there - my_first) * step_first}

    def second_peer(d):
        there = lax.rem(my_second + d, 4)
        return there, {"sp": sp, "dp": dp + (there - my_second) * step_second}

    barrier = pltpu.get_barrier_semaphore()

    def greet(device):
        pl.semaphore_signal(barrier, inc=1, device_id=device, device_id_type=MESH)

    def send(src, dst, send_sem, recv_sem, device):
        pltpu.make_async_remote_copy(
            src_ref=src, dst_ref=dst, send_sem=send_sem, recv_sem=recv_sem, device_id=device, device_id_type=MESH
        ).start()

    for d in range(1, 8):
        greet(member(d)[1])
    for d in range(1, 4):
        greet(first_peer(d)[1])
        greet(second_peer(d)[1])
        for t in range(4):
            greet({"sp": 2 * t + core, "dp": y * 4 + x + lax.rem(z_hi + d, 4) * 16})

    loads = [
        pltpu.make_async_copy(inputs_ref.at[sp], crop.at[sp], own_sem.at[0]),
        pltpu.make_async_copy(cotangent_ref.at[sp], upstream.at[sp], own_sem.at[1]),
        pltpu.make_async_copy(w_conv_any, w_conv, load_sem.at[0]),
        pltpu.make_async_copy(w_down_any, w_down, load_sem.at[1]),
        pltpu.make_async_copy(w_up_any, w_up, load_sem.at[2]),
    ]
    for load in loads:
        load.start()
    pl.semaphore_wait(barrier, 25)

    for d in range(1, 8):
        there, device = member(d)
        send(inputs_ref.at[there], crop.at[sp], crop_send, crop_recv.at[7 - d], device)
    for d in range(1, 8):
        there, device = member(d)
        send(cotangent_ref.at[there], upstream.at[sp], up_send, up_recv.at[7 - d], device)

    sibling = {"sp": sp + 1 - 2 * core, "dp": dp}

    def pair_start(q):
        for xx in range(4):
            src = rows.at[pl.ds(4 * q, 4), pl.ds(STARTS[xx] + 8 * (1 - core), 8)]
            send(src, pair_in.at[q, :, xx], pair_send.at[q], pair_recv.at[q], sibling)

    def pair_finish(q):
        group_wait(pair_in.at[q], pair_recv.at[q])
        for yy in range(4):
            for xx in range(4):
                own = rows[4 * q + yy, pl.ds(STARTS[xx] + 8 * core, 8)].astype(F32)
                total = own + pair_in[q, yy, xx].astype(F32)
                pair_sum[q, xx + core * (yy - xx), yy + core * (xx - yy)] = total.astype(BF)
        for d in range(1, 4):
            there, device = first_peer(d)
            send(pair_sum.at[q, there], first_in.at[q, 3 - d], first_send.at[q], first_recv.at[q], device)

    def first_finish(q):
        group_wait(first_in.at[q], first_recv.at[q])
        for s in range(4):
            total = pair_sum[q, my_first, s].astype(F32)
            for d in range(3):
                total = total + first_in[q, d, s].astype(F32)
            first_sum[q, s] = total.astype(BF)
        for d in range(1, 4):
            there, device = second_peer(d)
            send(first_sum.at[q, there], second_in.at[q, 3 - d], second_send.at[q], second_recv.at[q], device)

    def second_finish(q):
        group_wait(second_in.at[q], second_recv.at[q])
        total = first_sum[q, my_second].astype(F32)
        for d in range(3):
            total = total + second_in[q, d].astype(F32)
        second_sum[q] = total.astype(BF)
        for t in range(4):
            @pl.when(4 * q + t != z)
            def _():
                slot = lax.rem(z - (4 * q + t) + 16, 16) - 1
                send(
                    second_sum.at[q, pl.ds(2 * t, 2)], z_in.at[slot], z_send.at[q, t], z_recv,
                    {"sp": 2 * t + core, "dp": dp + (q - z_hi) * 16},
                )

    order_matrices(order, back, twice)
    columns[0:64, :] = jnp.zeros((64, 1152), BF)
    columns[576:640, :] = jnp.zeros((64, 1152), BF)
    padded[0:64, 0:128] = jnp.zeros((64, 128), BF)
    padded[576:640, 0:128] = jnp.zeros((64, 128), BF)
    padded[0:128, 128:256] = jnp.zeros((128, 128), BF)
    loads[2].wait()
    flip_weights(w_conv, w_flip)

    loads[0].wait()
    for d in range(7):
        group_wait(crop.at[0], crop_recv.at[d])
    hidden = forward(crop, w_conv, columns, slope)
    hid_taps = to_blocks(order[...], hidden)
    loads[3].wait()
    deep_act, deep_slope = deep_forward(hid_taps, w_down)
    turned[...] = columns[...].T

    loads[1].wait()
    for d in range(7):
        group_wait(upstream.at[0], up_recv.at[d])
    up_taps = to_blocks(order[...], upstream[...].reshape(512, 128))
    up_grads(rows, deep_act, up_taps)
    pair_start(3)
    loads[4].wait()
    grad_deep = deep_grads(up_taps, deep_slope, w_up)
    down_grads(rows, hid_taps, twice[...], grad_deep)
    pair_start(2)
    grad_pre_wide = pre_grads(upstream, grad_deep, w_down, back[...], slope)
    grad_pre = grad_pre_wide.astype(BF)
    conv_grads_late(rows, turned, padded, grad_pre)
    pair_start(1)
    conv_grads_early(rows, turned, grad_pre)
    pair_start(0)

    pair_finish(3)
    pair_finish(2)
    pair_finish(1)
    pair_finish(0)
    fill_columns(columns, grad_pre.astype(F32))
    grad_out[...] = convolve(columns, w_flip).astype(BF).reshape(8, 64, 128)
    for d in range(1, 8):
        there, device = member(d)
        send(grad_out.at[there], grad_input_ref.at[sp], grad_send, grad_recv.at[7 - d], device)
    own_grad = pltpu.make_async_copy(grad_out.at[sp], grad_input_ref.at[sp], own_sem.at[2])
    own_grad.start()
    for q in (3, 2, 1, 0):
        first_finish(q)
    for q in (3, 2, 1, 0):
        second_finish(q)

    group_wait(z_in, z_recv)
    total = second_sum[z_hi, pl.ds(2 * z_lo, 2)].astype(F32)
    for d in range(15):
        total = total + z_in[d].astype(F32)
    place = 4 * core + z_lo
    final[place] = total * scale
    for d in range(1, 8):
        send(final.at[place], final.at[place], out_send, out_recv, member(d)[1])
    group_wait(final.at[pl.ds(0, 7)], out_recv)
    whole = final[...].reshape(128, 128)
    for xx in range(4):
        @pl.when(x == xx)
        def _():
            share_ref[...] = whole[OFFSETS[xx] : OFFSETS[xx] + SHARE]

    own_grad.wait()
    for d in range(7):
        group_wait(grad_out.at[0], grad_recv.at[d])
    group_wait(crop.at[pl.ds(0, 7)], crop_send)
    group_wait(upstream.at[pl.ds(0, 7)], up_send)
    group_wait(grad_out.at[pl.ds(0, 7)], grad_send)
    for q in (3, 2, 1, 0):
        group_wait(pair_in.at[q], pair_send.at[q])
        group_wait(first_in.at[q], first_send.at[q])
        group_wait(second_in.at[q], second_send.at[q])
        for t in range(4):
            @pl.when(4 * q + t != z)
            def _():
                group_wait(z_in.at[0], z_send.at[q, t])
    group_wait(final.at[pl.ds(0, 7)], out_send)


def per_device(inputs, cotangent, w_conv, w_down, w_up):
    edge = inputs.shape[2]
    crops = inputs.shape[0] * lax.axis_size("dp")
    scale = 1.0 / math.sqrt(crops * edge * edge * edge)

    def kernel(*refs):
        step_kernel(scale, *refs)

    dma = pltpu.SemaphoreType.DMA
    vmem = pltpu.VMEM
    grad_input, share = pl.pallas_call(
        kernel,
        out_shape=(
            jax.ShapeDtypeStruct((8, 64, 128), BF),
            jax.ShapeDtypeStruct((SHARE, 128), F32),
        ),
        in_specs=[pl.BlockSpec(memory_space=pl.ANY)] * 5,
        out_specs=(pl.BlockSpec(memory_space=vmem), pl.BlockSpec(memory_space=vmem)),
        scratch_shapes=[
            vmem((8, 64, 128), BF),
            vmem((8, 64, 128), BF),
            vmem((3456, 128), BF),
            vmem((1024, 256), BF),
            vmem((2048, 128), BF),
            vmem((3456, 128), BF),
            vmem((640, 1152), BF),
            vmem((1152, 640), BF),
            vmem((640, 256), BF),
            vmem((512, 128), F32),
            vmem((128, 128), BF),
            vmem((128, 128), BF),
            vmem((128, 256), BF),
            vmem((16, TILES, 8, 128), BF),
            vmem((8, 64, 128), BF),
            vmem((4, 4, 4, 8, 8, 128), BF),
            vmem((4, 4, 4, 8, 8, 128), BF),
            vmem((4, 3, 4, 8, 8, 128), BF),
            vmem((4, 4, 8, 8, 128), BF),
            vmem((4, 3, 8, 8, 128), BF),
            vmem((4, 8, 8, 128), BF),
            vmem((15, 2, 8, 128), BF),
            vmem((8, 2, 8, 128), F32),
            dma((3,)), dma((3,)), dma, dma((7,)), dma, dma((7,)), dma, dma((7,)),
            dma((4,)), dma((4,)), dma((4,)), dma((4,)), dma((4,)), dma((4,)), dma((4, 4)), dma, dma, dma,
        ],
        compiler_params=pltpu.CompilerParams(
            collective_id=0, has_side_effects=True, vmem_limit_bytes=48 * 1024 * 1024
        ),
        name="whole_step",
    )(inputs.reshape(8, 64, 128), cotangent.reshape(8, 64, 128), w_conv, w_down, w_up)
    return (grad_input.reshape(inputs.shape), share.reshape(-1))


def solution(mesh):
    return jax.shard_map(
        per_device,
        mesh=mesh,
        in_specs=(P("dp", "sp", None, None, None), P("dp", "sp", None, None, None), P(), P(), P()),
        out_specs=(P("dp", "sp", None, None, None), P("dp")),
        check_vma=False,
    )
```

time: 92.6 us -> 60.3 us (0.65)
  starting transfers between devices: 18.8 us -> 0 us
  local copies, waits for them, and re-layouts: 24.8 us -> 6.34 us
  Pallas kernels: 36.6 us -> 53.1 us
  matrix products: 7.33 us -> 0 us
  waiting for transfers between devices: 2.71 us -> 0 us
    all_to_all x3 -> x0, starting transfers between devices: 18.8 us -> none  [the longest x1 10.3 us: per_device(): crop = lax.all_to_all(inputs, 'sp', split_axis=0, concat_axis=1, tiled=True)]
    pallas_call x1, Pallas kernels: 36.6 us -> 53.1 us  [per_device(): pl.pallas_call(kernel, out_shape=(jax.ShapeDtypeStruct((8, 64, 128), BF),...]
    unnamed x82 -> x12, local copies, waits for them, and re-layouts: 16.7 us -> 6.34 us
    dot_general x8 -> x0, matrix products: 7.33 us -> none  [the longest x1 3.14 us: per_device(): lax.dot_general(columns, grad_pre, (((0,), (0,)), ((), ())), preferred_el...]
    transpose x3 -> x0, local copies, waits for them, and re-layouts: 4.12 us -> none  [the longest x2 2.88 us: flip_taps(): return w_conv.reshape(27, width_in, width_in)[::-1].transpose(0, 2, 1).re...]
    slice x4 -> x0, local copies, waits for them, and re-layouts: 3.1 us -> none  [unfold_taps(): padded[:, i:i + size, j:j + size, k:k + size, :]]
    all_to_all x3 -> x0, waiting for transfers between devices: 2.71 us -> none  [the longest x1 1.71 us: per_device(): crop = lax.all_to_all(inputs, 'sp', split_axis=0, concat_axis=1, tiled=True)]
  transfers between devices with their start and end apart: 3 -> 0, of which waited for: 2 -> 0; matrix products, arithmetic and copies ran while one was open for 8% -> 0% of each run, Pallas kernels for 40% -> 0%
where the time goes in v2:
time: 60.3 us; the launch traced here: 60 us
  Pallas kernels  53.1 us (88%)
  local copies, waits for them, and re-layouts  6.34 us (11%)
  between operations  0.65 us (1%)
    pallas_call x1, Pallas kernels, per_device(): pl.pallas_call(kernel, out_shape=(jax.ShapeDtypeStruct((8, 64, 128), BF),...  53.1 us
    unnamed x12, local copies, waits for them, and re-layouts  6.34 us

profile of v2, /device:TPU:1, one launch (start us, length us, event | category | flops | bytes accessed | tf_op | source)
XLA Modules:
  0.0 60.0 jit_solution(2713277346137964975)
XLA Ops:
  0.6 0.0 copy-start
  0.6 1.2 %copy-done = bf16[3456,128]{1,0:T(8,128)(2,1)S(1)} copy-done((bf16[3456,128]{1,0:T(8,128)(2,1)S(1)}, bf16[3456,128]{1,0:T(8,128)(2,1)}, u32[]{:S(2)}) %copy-start) | copy-done | bytes 884760
  1.8 0.0 copy-start.1
  1.8 1.0 %copy-done.1 = bf16[1024,256]{1,0:T(8,128)(2,1)S(1)} copy-done((bf16[1024,256]{1,0:T(8,128)(2,1)S(1)}, bf16[1024,256]{1,0:T(8,128)(2,1)}, u32[]{:S(2)}) %copy-start.1) | copy-done | bytes 524312
  2.8 0.0 copy-start.2
  2.8 1.0 %copy-done.2 = bf16[2048,128]{1,0:T(8,128)(2,1)S(1)} copy-done((bf16[2048,128]{1,0:T(8,128)(2,1)S(1)}, bf16[2048,128]{1,0:T(8,128)(2,1)}, u32[]{:S(2)}) %copy-start.2) | copy-done | bytes 524312
  3.9 0.0 copy-start.3
  3.9 0.9 %copy-done.3 = bf16[8,1,8,8,128]{4,3,2,1,0:T(8,128)(2,1)S(1)} copy-done((bf16[8,1,8,8,128]{4,3,2,1,0:T(8,128)(2,1)S(1)}, bf16[8,1,8,8,128]{4,3,2,1,0:T(8,128)(2,1)}, u32[]{:S(2)}) %copy-start.3) | copy-done | bytes 131096
  4.8 0.0 copy-start.4
  4.8 0.9 %copy-done.4 = bf16[8,1,8,8,128]{4,3,2,1,0:T(8,128)(2,1)S(1)} copy-done((bf16[8,1,8,8,128]{4,3,2,1,0:T(8,128)(2,1)S(1)}, bf16[8,1,8,8,128]{4,3,2,1,0:T(8,128)(2,1)}, u32[]{:S(2)}) %copy-start.4) | copy-done | bytes 131096
  5.7 53.1 %whole_step.1 = (bf16[8,64,128]{2,1,0:T(8,128)(2,1)S(1)}, f32[118,128]{1,0:T(8,128)S(1)}) custom-call(bf16[8,64,128]{2,1,0:T(8,128)(2,1)S(1)} %bitcast.6, bf16[8,64,128]{2,1,0:T(8,128)(2,1)S(1)} %bitcast.7, bf16[3456,128]{1,0:T(8,128)(2,1)S(1)} %copy-done, bf16[1024,256]{1,0:T(8,128)(2,1)S(1)} %copy-done.1, bf16[2048,128]{1,0:T(8,128)(2,1)S(1)} %copy-done.2), custom_call_target="tpu_custom_call" | custom-call | tf_op jit(solution)/shard_map/whole_step/pallas_call | solution.py:386
  58.8 0.7 %copy.10 = bf16[8,1,8,8,128]{4,3,2,1,0:T(8,128)(2,1)} copy(bf16[8,1,8,8,128]{4,3,2,1,0:T(8,128)(2,1)S(1)} %bitcast.8) | data formatting | bytes 262144
  59.4 0.6 %copy.11 = f32[15104]{0:T(1024)} copy(f32[15104]{0:T(1024)S(1)} %bitcast.9) | data formatting | bytes 120832
Async XLA Ops:
  0.6 1.2 %copy-start = (bf16[3456,128]{1,0:T(8,128)(2,1)S(1)}, bf16[3456,128]{1,0:T(8,128)(2,1)}, u32[]{:S(2)}) copy-start(bf16[3456,128]{1,0:T(8,128)(2,1)} %refs_2_.1) | copy-start | bytes 2654212
  1.8 1.0 %copy-start.1 = (bf16[1024,256]{1,0:T(8,128)(2,1)S(1)}, bf16[1024,256]{1,0:T(8,128)(2,1)}, u32[]{:S(2)}) copy-start(bf16[1024,256]{1,0:T(8,128)(2,1)} %refs_3_.1) | copy-start | bytes 1572868
  2.8 1.0 %copy-start.2 = (bf16[2048,128]{1,0:T(8,128)(2,1)S(1)}, bf16[2048,128]{1,0:T(8,128)(2,1)}, u32[]{:S(2)}) copy-start(bf16[2048,128]{1,0:T(8,128)(2,1)} %refs_4_.1) | copy-start | bytes 1572868
  3.9 0.9 %copy-start.3 = (bf16[8,1,8,8,128]{4,3,2,1,0:T(8,128)(2,1)S(1)}, bf16[8,1,8,8,128]{4,3,2,1,0:T(8,128)(2,1)}, u32[]{:S(2)}) copy-start(bf16[8,1,8,8,128]{4,3,2,1,0:T(8,128)(2,1)} %param.5) | copy-start | bytes 393220
  4.8 0.9 %copy-start.4 = (bf16[8,1,8,8,128]{4,3,2,1,0:T(8,128)(2,1)S(1)}, bf16[8,1,8,8,128]{4,3,2,1,0:T(8,128)(2,1)}, u32[]{:S(2)}) copy-start(bf16[8,1,8,8,128]{4,3,2,1,0:T(8,128)(2,1)} %param.6) | copy-start | bytes 393220

commit v3 on v2

--- a/solution.py
+++ b/solution.py
@@ -52,40 +52,49 @@
         w_flip_ref[128 * t : 128 * (t + 1), :] = block.astype(F32).T.astype(BF)
 
 
-def fill_columns(columns_ref, volume):
-    lines = volume.reshape(64, 8, 128)
-    k_at = lax.broadcasted_iota(jnp.int32, (64, 8, 128), 1)
-    zero_line = jnp.zeros((8, 1, 8, 128), F32)
+def fill_columns(columns_ref, first, planes):
+    count = planes.shape[0] // 64
+    lines = planes.reshape(8 * count, 8, 128)
+    k_at = lax.broadcasted_iota(jnp.int32, (8 * count, 8, 128), 1)
+    zero_line = jnp.zeros((count, 1, 8, 128), F32)
     for k in range(3):
         moved = lines
         if k == 0:
             moved = jnp.where(k_at == 0, 0.0, pltpu.roll(lines, 1, axis=1))
         if k == 2:
             moved = jnp.where(k_at == 7, 0.0, pltpu.roll(lines, 7, axis=1))
-        planes = moved.reshape(8, 8, 8, 128)
+        moved = moved.reshape(count, 8, 8, 128)
         for j in range(3):
-            shifted = planes
+            shifted = moved
             if j == 0:
-                shifted = jnp.concatenate([zero_line, planes[:, :7]], axis=1)
+                shifted = jnp.concatenate([zero_line, moved[:, :7]], axis=1)
             if j == 2:
-                shifted = jnp.concatenate([planes[:, 1:], zero_line], axis=1)
+                shifted = jnp.concatenate([moved[:, 1:], zero_line], axis=1)
             lane = 128 * (3 * j + k)
-            columns_ref[64:576, lane : lane + 128] = shifted.reshape(512, 128).astype(BF)
-
-
-def convolve(columns_ref, weights_ref):
-    total = dot(columns_ref[0:512, :], weights_ref[0:1152, :])
-    total += dot(columns_ref[64:576, :], weights_ref[1152:2304, :])
-    total += dot(columns_ref[128:640, :], weights_ref[2304:3456, :])
-    return total
+            columns_ref[first : first + 64 * count, lane : lane + 128] = shifted.reshape(64 * count, 128).astype(BF)
+
+
+def fill_plane(columns_ref, field_ref, plane, count=1):
+    values = field_ref[plane : plane + count].reshape(256 * count, 128).astype(F32)
+    fill_columns(columns_ref, 256 * plane, values)
+
+
+def tap_dot(columns_ref, weights_ref, i):
+    return dot(columns_ref[256 * i : 256 * i + 512, :], weights_ref[1152 * i : 1152 * (i + 1), :])
 
 
 def to_blocks(order, volume):
-    side_by_side = jnp.concatenate([volume[128 * a : 128 * (a + 1)] for a in range(4)], axis=1)
+    side_by_side = jnp.concatenate(
+        [
+            jnp.concatenate([volume[64 * c : 64 * c + 64], volume[64 * c + 256 : 64 * c + 320]], axis=0)
+            for c in range(4)
+        ],
+        axis=1,
+    )
     moved = dot(order, side_by_side).astype(BF)
     return [
         jnp.concatenate(
-            [moved[16 * t : 16 * (t + 1), 128 * a : 128 * (a + 1)] for a in range(4)], axis=0
+            [moved[16 * t : 16 * (t + 1), 128 * c : 128 * (c + 1)] for c in range(4)], axis=0
         )
         for t in range(8)
     ]
@@ -95,14 +104,16 @@
     stacked = jnp.concatenate(
         [
             jnp.concatenate(
-                [blocks[16 * a : 16 * (a + 1), 128 * t : 128 * (t + 1)] for a in range(4)], axis=1
+                [blocks[16 * c : 16 * (c + 1), 128 * t : 128 * (t + 1)] for c in range(4)], axis=1
             )
             for t in range(8)
         ],
         axis=0,
     )
     moved = dot(back, stacked)
-    return jnp.concatenate([moved[:, 128 * a : 128 * (a + 1)] for a in range(4)], axis=0)
+    return jnp.concatenate(
+        [moved[64 * p : 64 * (p + 1), 128 * c : 128 * (c + 1)] for p in range(2) for c in range(4)], axis=0
+    )
 
 
 def put_rows(rows_ref, tile, values):
@@ -121,13 +132,6 @@
     return pre * s, s * (1.0 + pre * (1.0 - s))
 
 
-def forward(crop_ref, w_conv_ref, columns_ref, slope_ref):
-    fill_columns(columns_ref, crop_ref[...].reshape(512, 128).astype(F32))
-    hidden, slope = logistic_parts(convolve(columns_ref, w_conv_ref))
-    slope_ref[...] = slope
-    return hidden.astype(BF)
-
-
 def deep_forward(hid_taps, w_down_ref):
     pre_deep = dot(jnp.concatenate(hid_taps, axis=1), w_down_ref[...])
     act, slope = logistic_parts(pre_deep)
@@ -160,16 +164,8 @@
     return summed * slope_ref[...]
 
 
-def conv_grads_late(rows_ref, turned_ref, padded_ref, grad_pre):
-    padded_ref[64:576, 0:128] = grad_pre
-    padded_ref[128:640, 128:256] = grad_pre
-    total = dot(turned_ref[...], padded_ref[...])
-    for i in (1, 2):
-        put_rows(rows_ref, 144 * i, total[:, 128 * (i - 1) : 128 * i])
-
-
-def conv_grads_early(rows_ref, turned_ref, grad_pre):
-    put_rows(rows_ref, 0, dot(turned_ref[:, 0:512], grad_pre))
+def conv_grads(rows_ref, turned_ref, grad_pre, i):
+    put_rows(rows_ref, 144 * i, dot(turned_ref[:, 256 * i : 256 * i + 512], grad_pre))
 
 
 def group_wait(ref, sem):
@@ -180,9 +176,10 @@
     scale,
     inputs_ref, cotangent_ref, w_conv_any, w_down_any, w_up_any,
     grad_input_ref, share_ref,
-    crop, upstream, w_conv, w_down, w_up, w_flip, columns, turned, padded, slope, order, back, twice, rows, grad_out,
+    field, upstream, w_conv, w_down, w_up, w_flip, columns, turned, slope, order, back, twice, rows,
+    grad_field, grad_out,
     pair_in, pair_sum, first_in, first_sum, second_in, second_sum, z_in, final,
-    load_sem, own_sem, crop_send, crop_recv, up_send, up_recv, grad_send, grad_recv,
+    load_sem, own_sem, near_send, near_recv, low_recv, high_recv, halo_send, halo_low, halo_high, grad_send, grad_recv,
     pair_send, pair_recv, first_send, first_recv, second_send, second_recv, z_send, z_recv, out_send, out_recv,
 ):
     sp = lax.axis_index("sp")
@@ -228,25 +225,49 @@
         for t in range(4):
             greet({"sp": 2 * t + core, "dp": y * 4 + x + lax.rem(z_hi + d, 4) * 16})
 
+    own_crops = pl.ds(4 * core, 4)
+    far_crops = pl.ds(4 * (1 - core), 4)
+    sibling = {"sp": sp + 1 - 2 * core, "dp": dp}
+    side = z_lo - 1 + 2 * core
+    has_side = jnp.logical_and(side >= 0, side <= 3)
     loads = [
-        pltpu.make_async_copy(inputs_ref.at[sp], crop.at[sp], own_sem.at[0]),
-        pltpu.make_async_copy(cotangent_ref.at[sp], upstream.at[sp], own_sem.at[1]),
+        pltpu.make_async_copy(inputs_ref.at[own_crops], field.at[1 + core], own_sem.at[0]),
+        pltpu.make_async_copy(cotangent_ref.at[own_crops], upstream.at[core], own_sem.at[1]),
         pltpu.make_async_copy(w_conv_any, w_conv, load_sem.at[0]),
         pltpu.make_async_copy(w_down_any, w_down, load_sem.at[1]),
         pltpu.make_async_copy(w_up_any, w_up, load_sem.at[2]),
     ]
     for load in loads:
         load.start()
+
+    @pl.when(z_lo == 0)
+    def _():
+        field[0] = jnp.zeros((4, 64, 128), BF)
+        grad_field[0] = jnp.zeros((4, 64, 128), BF)
+
+    @pl.when(z_lo == 3)
+    def _():
+        field[3] = jnp.zeros((4, 64, 128), BF)
+        grad_field[3] = jnp.zeros((4, 64, 128), BF)
+
     pl.semaphore_wait(barrier, 25)
 
-    for d in range(1, 8):
-        there, device = member(d)
-        send(inputs_ref.at[there], crop.at[sp], crop_send, crop_recv.at[7 - d], device)
-    for d in range(1, 8):
-        there, device = member(d)
-        send(cotangent_ref.at[there], upstream.at[sp], up_send, up_recv.at[7 - d], device)
-
-    sibling = {"sp": sp + 1 - 2 * core, "dp": dp}
+    @pl.when(core == 0)
+    def _():
+        @pl.when(z_lo > 0)
+        def _():
+            for c in range(2):
+                send(inputs_ref.at[pl.ds(4 * c, 4)], field.at[3], near_send.at[1 + c], high_recv, {"sp": sp - 2 + c, "dp": dp})
+
+    @pl.when(core == 1)
+    def _():
+        @pl.when(z_lo < 3)
+        def _():
+            for c in range(2):
+                send(inputs_ref.at[pl.ds(4 * c, 4)], field.at[0], near_send.at[1 + c], low_recv, {"sp": sp + 1 + c, "dp": dp})
+
+    send(inputs_ref.at[far_crops], field.at[1 + core], near_send.at[0], near_recv.at[0], sibling)
+    send(cotangent_ref.at[far_crops], upstream.at[core], near_send.at[3], near_recv.at[1], sibling)
 
     def pair_start(q):
         for xx in range(4):
@@ -291,26 +312,35 @@
                 )
 
     order_matrices(order, back, twice)
-    columns[0:64, :] = jnp.zeros((64, 1152), BF)
-    columns[576:640, :] = jnp.zeros((64, 1152), BF)
-    padded[0:64, 0:128] = jnp.zeros((64, 128), BF)
-    padded[576:640, 0:128] = jnp.zeros((64, 128), BF)
-    padded[0:128, 128:256] = jnp.zeros((128, 128), BF)
     loads[2].wait()
     flip_weights(w_conv, w_flip)
 
     loads[0].wait()
-    for d in range(7):
-        group_wait(crop.at[0], crop_recv.at[d])
-    hidden = forward(crop, w_conv, columns, slope)
-    hid_taps = to_blocks(order[...], hidden)
+    group_wait(field.at[0], near_recv.at[0])
+    fill_plane(columns, field, 1, 2)
+    pre_conv = tap_dot(columns, w_conv, 1)
+    turned[:, 256:768] = columns[256:768, :].T
+
+    @pl.when(z_lo > 0)
+    def _():
+        group_wait(field.at[0], low_recv)
+
+    @pl.when(z_lo < 3)
+    def _():
+        group_wait(field.at[3], high_recv)
+
+    fill_plane(columns, field, 0)
+    fill_plane(columns, field, 3)
+    pre_conv += tap_dot(columns, w_conv, 0)
+    pre_conv += tap_dot(columns, w_conv, 2)
+    hidden, pre_slope = logistic_parts(pre_conv)
+    slope[...] = pre_slope
+    hid_taps = to_blocks(order[...], hidden.astype(BF))
     loads[3].wait()
     deep_act, deep_slope = deep_forward(hid_taps, w_down)
-    turned[...] = columns[...].T
 
     loads[1].wait()
-    for d in range(7):
-        group_wait(upstream.at[0], up_recv.at[d])
+    group_wait(upstream.at[0], near_recv.at[1])
     up_taps = to_blocks(order[...], upstream[...].reshape(512, 128))
     up_grads(rows, deep_act, up_taps)
     pair_start(3)
@@ -318,26 +348,52 @@
     grad_deep = deep_grads(up_taps, deep_slope, w_up)
     down_grads(rows, hid_taps, twice[...], grad_deep)
     pair_start(2)
-    grad_pre_wide = pre_grads(upstream, grad_deep, w_down, back[...], slope)
-    grad_pre = grad_pre_wide.astype(BF)
-    conv_grads_late(rows, turned, padded, grad_pre)
+    grad_pre = pre_grads(upstream, grad_deep, w_down, back[...], slope).astype(BF)
+    grad_field[1:3] = grad_pre.reshape(2, 4, 64, 128)
+
+    @pl.when(z_lo > 0)
+    def _():
+        send(grad_field.at[1], grad_field.at[3], halo_send.at[0], halo_high, {"sp": sp - 2, "dp": dp})
+
+    @pl.when(z_lo < 3)
+    def _():
+        send(grad_field.at[2], grad_field.at[0], halo_send.at[1], halo_low, {"sp": sp + 2, "dp": dp})
+
+    turned[:, 0:256] = columns[0:256, :].T
+    turned[:, 768:1024] = columns[768:1024, :].T
+    conv_grads(rows, turned, grad_pre, 2)
+    conv_grads(rows, turned, grad_pre, 1)
     pair_start(1)
-    conv_grads_early(rows, turned, grad_pre)
+    pair_finish(3)
+    conv_grads(rows, turned, grad_pre, 0)
     pair_start(0)
 
-    pair_finish(3)
     pair_finish(2)
+    fill_plane(columns, grad_field, 1, 2)
     pair_finish(1)
     pair_finish(0)
-    fill_columns(columns, grad_pre.astype(F32))
-    grad_out[...] = convolve(columns, w_flip).astype(BF).reshape(8, 64, 128)
-    for d in range(1, 8):
-        there, device = member(d)
-        send(grad_out.at[there], grad_input_ref.at[sp], grad_send, grad_recv.at[7 - d], device)
-    own_grad = pltpu.make_async_copy(grad_out.at[sp], grad_input_ref.at[sp], own_sem.at[2])
+    first_finish(3)
+
+    @pl.when(z_lo > 0)
+    def _():
+        group_wait(grad_field.at[0], halo_low)
+
+    @pl.when(z_lo < 3)
+    def _():
+        group_wait(grad_field.at[3], halo_high)
+
+    fill_plane(columns, grad_field, 0)
+    fill_plane(columns, grad_field, 3)
+    total = tap_dot(columns, w_flip, 0)
+    total += tap_dot(columns, w_flip, 1)
+    total += tap_dot(columns, w_flip, 2)
+    grad_out[...] = total.astype(BF).reshape(2, 4, 64, 128)
+    first_finish(2)
+    first_finish(1)
+    first_finish(0)
+    send(grad_out.at[1 - core], grad_input_ref.at[own_crops], grad_send, grad_recv, sibling)
+    own_grad = pltpu.make_async_copy(grad_out.at[core], grad_input_ref.at[own_crops], own_sem.at[2])
     own_grad.start()
-    for q in (3, 2, 1, 0):
-        first_finish(q)
     for q in (3, 2, 1, 0):
         second_finish(q)
 
@@ -357,11 +413,24 @@
             share_ref[...] = whole[OFFSETS[xx] : OFFSETS[xx] + SHARE]
 
     own_grad.wait()
-    for d in range(7):
-        group_wait(grad_out.at[0], grad_recv.at[d])
-    group_wait(crop.at[pl.ds(0, 7)], crop_send)
-    group_wait(upstream.at[pl.ds(0, 7)], up_send)
-    group_wait(grad_out.at[pl.ds(0, 7)], grad_send)
+    group_wait(grad_out.at[0], grad_recv)
+    group_wait(grad_out.at[0], grad_send)
+    group_wait(field.at[0], near_send.at[0])
+    group_wait(field.at[0], near_send.at[3])
+
+    @pl.when(has_side)
+    def _():
+        group_wait(field.at[0], near_send.at[1])
+        group_wait(field.at[0], near_send.at[2])
+
+    @pl.when(z_lo > 0)
+    def _():
+        group_wait(grad_field.at[0], halo_send.at[0])
+
+    @pl.when(z_lo < 3)
+    def _():
+        group_wait(grad_field.at[0], halo_send.at[1])
+
     for q in (3, 2, 1, 0):
         group_wait(pair_in.at[q], pair_send.at[q])
         group_wait(first_in.at[q], first_send.at[q])
@@ -392,21 +461,21 @@
         in_specs=[pl.BlockSpec(memory_space=pl.ANY)] * 5,
         out_specs=(pl.BlockSpec(memory_space=vmem), pl.BlockSpec(memory_space=vmem)),
         scratch_shapes=[
-            vmem((8, 64, 128), BF),
-            vmem((8, 64, 128), BF),
+            vmem((4, 4, 64, 128), BF),
+            vmem((2, 4, 64, 128), BF),
             vmem((3456, 128), BF),
             vmem((1024, 256), BF),
             vmem((2048, 128), BF),
             vmem((3456, 128), BF),
-            vmem((640, 1152), BF),
-            vmem((1152, 640), BF),
-            vmem((640, 256), BF),
+            vmem((1024, 1152), BF),
+            vmem((1152, 1024), BF),
             vmem((512, 128), F32),
             vmem((128, 128), BF),
             vmem((128, 128), BF),
             vmem((128, 256), BF),
             vmem((16, TILES, 8, 128), BF),
-            vmem((8, 64, 128), BF),
+            vmem((4, 4, 64, 128), BF),
+            vmem((2, 4, 64, 128), BF),
             vmem((4, 4, 4, 8, 8, 128), BF),
             vmem((4, 4, 4, 8, 8, 128), BF),
             vmem((4, 3, 4, 8, 8, 128), BF),
@@ -415,11 +484,11 @@
             vmem((4, 8, 8, 128), BF),
             vmem((15, 2, 8, 128), BF),
             vmem((8, 2, 8, 128), F32),
-            dma((3,)), dma((3,)), dma, dma((7,)), dma, dma((7,)), dma, dma((7,)),
+            dma((3,)), dma((3,)), dma((4,)), dma((2,)), dma, dma, dma((2,)), dma, dma, dma, dma,
             dma((4,)), dma((4,)), dma((4,)), dma((4,)), dma((4,)), dma((4,)), dma((4, 4)), dma, dma, dma,
         ],
         compiler_params=pltpu.CompilerParams(
-            collective_id=0, has_side_effects=True, vmem_limit_bytes=48 * 1024 * 1024
+            collective_id=0, has_side_effects=True, vmem_limit_bytes=55040 * 1024
         ),
         name="whole_step",
     )(inputs.reshape(8, 64, 128), cotangent.reshape(8, 64, 128), w_conv, w_down, w_up)

time: 60.3 us -> 50.7 us (0.84)
  local copies, waits for them, and re-layouts: 6.34 us -> 1.29 us
  Pallas kernels: 53.1 us -> 48.7 us
    unnamed x12 -> x2, local copies, waits for them, and re-layouts: 6.34 us -> 1.29 us
    pallas_call x1, Pallas kernels: 53.1 us -> 48.7 us  [per_device(): pl.pallas_call(kernel, out_shape=(jax.ShapeDtypeStruct((8, 64, 128), BF),...]
where the time goes in v3:
time: 50.7 us; the launch traced here: 50.6 us
  Pallas kernels  48.7 us (96%)
  local copies, waits for them, and re-layouts  1.29 us (3%)
  between operations  0.64 us (1%)
    pallas_call x1, Pallas kernels, per_device(): pl.pallas_call(kernel, out_shape=(jax.ShapeDtypeStruct((8, 64, 128), BF),...  48.7 us
    unnamed x2, local copies, waits for them, and re-layouts  1.29 us

profile of v3, /device:TPU:1, one launch (start us, length us, event | category | flops | bytes accessed | tf_op | source)
XLA Modules:
  0.0 50.6 jit_solution(5450952952674140487)
XLA Ops:
  0.6 48.7 %whole_step.1 = (bf16[8,64,128]{2,1,0:T(8,128)(2,1)S(1)}, f32[118,128]{1,0:T(8,128)S(1)}) custom-call(bf16[8,64,128]{2,1,0:T(8,128)(2,1)} %bitcast.8, bf16[8,64,128]{2,1,0:T(8,128)(2,1)} %bitcast.9, bf16[3456,128]{1,0:T(8,128)(2,1)} %refs_2_.1, bf16[1024,256]{1,0:T(8,128)(2,1)} %refs_3_.1, bf16[2048,128]{1,0:T(8,128)(2,1)} %refs_4_.1), custom_call_target="tpu_custom_call" | custom-call | tf_op jit(solution)/shard_map/whole_step/pallas_call | solution.py:455
  49.3 0.7 %copy.10 = bf16[8,1,8,8,128]{4,3,2,1,0:T(8,128)(2,1)} copy(bf16[8,1,8,8,128]{4,3,2,1,0:T(8,128)(2,1)S(1)} %bitcast.6) | data formatting | bytes 262144
  50.0 0.6 %copy.11 = f32[15104]{0:T(1024)} copy(f32[15104]{0:T(1024)S(1)} %bitcast.7) | data formatting | bytes 120832

commit v4 on v3

--- a/solution.py
+++ b/solution.py
@@ -217,13 +217,22 @@
             src_ref=src, dst_ref=dst, send_sem=send_sem, recv_sem=recv_sem, device_id=device, device_id_type=MESH
         ).start()
 
+    at_end = jnp.logical_or(z_lo == 0, z_lo == 3)
+
+    def along_z(offset):
+        there = lax.rem(z + offset + 16, 16)
+        return {"sp": 2 * lax.rem(there, 4) + core, "dp": dp + (lax.div(there, 4) - z_hi) * 16}
+
+    for place, offsets in enumerate(((-6, -5, -4, -3, -2, -1, 4), (-6, -2, 3), (6, 2, -3), (6, 5, 4, 3, 2, 1, -4))):
+        @pl.when(z_lo == place)
+        def _():
+            for offset in offsets:
+                greet(along_z(offset))
     for d in range(1, 8):
         greet(member(d)[1])
     for d in range(1, 4):
         greet(first_peer(d)[1])
         greet(second_peer(d)[1])
-        for t in range(4):
-            greet({"sp": 2 * t + core, "dp": y * 4 + x + lax.rem(z_hi + d, 4) * 16})
 
     own_crops = pl.ds(4 * core, 4)
     far_crops = pl.ds(4 * (1 - core), 4)
@@ -250,7 +259,7 @@
         field[3] = jnp.zeros((4, 64, 128), BF)
         grad_field[3] = jnp.zeros((4, 64, 128), BF)
 
-    pl.semaphore_wait(barrier, 25)
+    pl.semaphore_wait(barrier, 16 + 2 * (z_lo - 1) * (z_lo - 2))
 
     @pl.when(core == 0)
     def _():
@@ -268,6 +277,12 @@
 
     send(inputs_ref.at[far_crops], field.at[1 + core], near_send.at[0], near_recv.at[0], sibling)
     send(cotangent_ref.at[far_crops], upstream.at[core], near_send.at[3], near_recv.at[1], sibling)
+
+    def goes_low(place):
+        return jnp.logical_or(place == 1, place >= 10)
+
+    def goes_high(place):
+        return jnp.logical_or(place == 2, jnp.logical_and(place >= 4, place <= 9))
 
     def pair_start(q):
         for xx in range(4):
@@ -302,14 +317,18 @@
         for d in range(3):
             total = total + second_in[q, d].astype(F32)
         second_sum[q] = total.astype(BF)
-        for t in range(4):
-            @pl.when(4 * q + t != z)
-            def _():
-                slot = lax.rem(z - (4 * q + t) + 16, 16) - 1
-                send(
-                    second_sum.at[q, pl.ds(2 * t, 2)], z_in.at[slot], z_send.at[q, t], z_recv,
-                    {"sp": 2 * t + core, "dp": dp + (q - z_hi) * 16},
-                )
+        place = lax.rem(z - 4 * q + 16, 16)
+        there = dp + (q - z_hi) * 16
+
+        @pl.when(goes_low(place))
+        def _():
+            slot = lax.rem(place + 7, 8) * lax.div(place, 10)
+            send(second_sum.at[q], z_in.at[slot], z_send.at[q], z_recv, {"sp": core, "dp": there})
+
+        @pl.when(goes_high(place))
+        def _():
+            slot = (place - 3) * lax.div(place + 12, 16)
+            send(second_sum.at[q], z_in.at[slot], z_send.at[q], z_recv, {"sp": 6 + core, "dp": there})
 
     order_matrices(order, back, twice)
     loads[2].wait()
@@ -372,7 +391,6 @@
     fill_plane(columns, grad_field, 1, 2)
     pair_finish(1)
     pair_finish(0)
-    first_finish(3)
 
     @pl.when(z_lo > 0)
     def _():
@@ -388,25 +406,31 @@
     total += tap_dot(columns, w_flip, 1)
     total += tap_dot(columns, w_flip, 2)
     grad_out[...] = total.astype(BF).reshape(2, 4, 64, 128)
-    first_finish(2)
-    first_finish(1)
-    first_finish(0)
+    for q in (3, 2, 1, 0):
+        first_finish(q)
     send(grad_out.at[1 - core], grad_input_ref.at[own_crops], grad_send, grad_recv, sibling)
     own_grad = pltpu.make_async_copy(grad_out.at[core], grad_input_ref.at[own_crops], own_sem.at[2])
     own_grad.start()
     for q in (3, 2, 1, 0):
         second_finish(q)
 
-    group_wait(z_in, z_recv)
-    total = second_sum[z_hi, pl.ds(2 * z_lo, 2)].astype(F32)
-    for d in range(15):
-        total = total + z_in[d].astype(F32)
-    place = 4 * core + z_lo
-    final[place] = total * scale
-    for d in range(1, 8):
-        send(final.at[place], final.at[place], out_send, out_recv, member(d)[1])
-    group_wait(final.at[pl.ds(0, 7)], out_recv)
-    whole = final[...].reshape(128, 128)
+    @pl.when(at_end)
+    def _():
+        group_wait(z_in, z_recv)
+        total = second_sum[z_hi].astype(F32)
+        for d in range(7):
+            total = total + z_in[d].astype(F32)
+        end = lax.div(z_lo, 3)
+        final[end, core] = total.astype(BF)
+        for d in range(1, 8):
+            send(final.at[end, core], final.at[end, core], out_send, out_recv, member(d)[1])
+        group_wait(z_in.at[pl.ds(0, 3)], out_recv)
+
+    @pl.when(jnp.logical_not(at_end))
+    def _():
+        group_wait(z_in.at[pl.ds(0, 4)], out_recv)
+
+    whole = (final[0].astype(F32) + final[1].astype(F32)).reshape(128, 128) * scale
     for xx in range(4):
         @pl.when(x == xx)
         def _():
@@ -435,11 +459,15 @@
         group_wait(pair_in.at[q], pair_send.at[q])
         group_wait(first_in.at[q], first_send.at[q])
         group_wait(second_in.at[q], second_send.at[q])
-        for t in range(4):
-            @pl.when(4 * q + t != z)
-            def _():
-                group_wait(z_in.at[0], z_send.at[q, t])
-    group_wait(final.at[pl.ds(0, 7)], out_send)
+        place = lax.rem(z - 4 * q + 16, 16)
+
+        @pl.when(jnp.logical_or(goes_low(place), goes_high(place)))
+        def _():
+            group_wait(z_in.at[0], z_send.at[q])
+
+    @pl.when(at_end)
+    def _():
+        group_wait(z_in, out_send)
 
 
 def per_device(inputs, cotangent, w_conv, w_down, w_up):
@@ -482,10 +510,10 @@
             vmem((4, 4, 8, 8, 128), BF),
             vmem((4, 3, 8, 8, 128), BF),
             vmem((4, 8, 8, 128), BF),
-            vmem((15, 2, 8, 128), BF),
-            vmem((8, 2, 8, 128), F32),
+            vmem((7, 8, 8, 128), BF),
+            vmem((2, 2, 8, 8, 128), BF),
             dma((3,)), dma((3,)), dma((4,)), dma((2,)), dma, dma, dma((2,)), dma, dma, dma, dma,
-            dma((4,)), dma((4,)), dma((4,)), dma((4,)), dma((4,)), dma((4,)), dma((4, 4)), dma, dma, dma,
+            dma((4,)), dma((4,)), dma((4,)), dma((4,)), dma((4,)), dma((4,)), dma((4,)), dma, dma, dma,
         ],
         compiler_params=pltpu.CompilerParams(
             collective_id=0, has_side_effects=True, vmem_limit_bytes=55040 * 1024

time: 50.7 us -> 48.8 us (0.963)
  Pallas kernels: 48.7 us -> 46.8 us
    pallas_call x1, Pallas kernels: 48.7 us -> 46.8 us  [per_device(): pl.pallas_call(kernel, out_shape=(jax.ShapeDtypeStruct((8, 64, 128), BF),...]
where the time goes in v4:
time: 48.8 us; the launch traced here: 48.7 us
  Pallas kernels  46.8 us (96%)
  local copies, waits for them, and re-layouts  1.29 us (3%)
  between operations  0.64 us (1%)
    pallas_call x1, Pallas kernels, per_device(): pl.pallas_call(kernel, out_shape=(jax.ShapeDtypeStruct((8, 64, 128), BF),...  46.8 us
    unnamed x2, local copies, waits for them, and re-layouts  1.29 us

profile of v4, /device:TPU:1, one launch (start us, length us, event | category | flops | bytes accessed | tf_op | source)
XLA Modules:
  0.0 48.7 jit_solution(17731230507786389086)
XLA Ops:
  0.6 46.8 %whole_step.1 = (bf16[8,64,128]{2,1,0:T(8,128)(2,1)S(1)}, f32[118,128]{1,0:T(8,128)S(1)}) custom-call(bf16[8,64,128]{2,1,0:T(8,128)(2,1)} %bitcast.8, bf16[8,64,128]{2,1,0:T(8,128)(2,1)} %bitcast.9, bf16[3456,128]{1,0:T(8,128)(2,1)} %refs_2_.1, bf16[1024,256]{1,0:T(8,128)(2,1)} %refs_3_.1, bf16[2048,128]{1,0:T(8,128)(2,1)} %refs_4_.1), custom_call_target="tpu_custom_call" | custom-call | tf_op jit(solution)/shard_map/whole_step/pallas_call | solution.py:483
  47.4 0.7 %copy.10 = bf16[8,1,8,8,128]{4,3,2,1,0:T(8,128)(2,1)} copy(bf16[8,1,8,8,128]{4,3,2,1,0:T(8,128)(2,1)S(1)} %bitcast.6) | data formatting | bytes 262144
  48.1 0.6 %copy.11 = f32[15104]{0:T(1024)} copy(f32[15104]{0:T(1024)S(1)} %bitcast.7) | data formatting | bytes 120832

commit v5 on v4

--- a/solution.py
+++ b/solution.py
@@ -190,22 +190,21 @@
     y = lax.rem(lax.div(dp, 4), 4)
     x = lax.rem(dp, 4)
     z = z_hi * 4 + z_lo
-    my_first = x + core * (y - x)
-    my_second = y + core * (x - y)
-    step_first = 1 + 3 * core
-    step_second = 4 - 3 * core
+    turns = [core, 1 - core, core, 1 - core]
+    my_first = [x + turn * (y - x) for turn in turns]
+    my_second = [y + turn * (x - y) for turn in turns]
 
     def member(d):
         there = lax.rem(sp + d, 8)
         return there, {"sp": there, "dp": dp}
 
-    def first_peer(d):
-        there = lax.rem(my_first + d, 4)
-        return there, {"sp": sp, "dp": dp + (there - my_first) * step_first}
-
-    def second_peer(d):
-        there = lax.rem(my_second + d, 4)
-        return there, {"sp": sp, "dp": dp + (there - my_second) * step_second}
+    def first_peer(q, d):
+        there = lax.rem(my_first[q] + d, 4)
+        return there, {"sp": sp, "dp": dp + (there - my_first[q]) * (1 + 3 * turns[q])}
+
+    def second_peer(q, d):
+        there = lax.rem(my_second[q] + d, 4)
+        return there, {"sp": sp, "dp": dp + (there - my_second[q]) * (4 - 3 * turns[q])}
 
     barrier = pltpu.get_barrier_semaphore()
 
@@ -231,8 +230,8 @@
     for d in range(1, 8):
         greet(member(d)[1])
     for d in range(1, 4):
-        greet(first_peer(d)[1])
-        greet(second_peer(d)[1])
+        greet(first_peer(0, d)[1])
+        greet(second_peer(0, d)[1])
 
     own_crops = pl.ds(4 * core, 4)
     far_crops = pl.ds(4 * (1 - core), 4)
@@ -295,25 +294,25 @@
             for xx in range(4):
                 own = rows[4 * q + yy, pl.ds(STARTS[xx] + 8 * core, 8)].astype(F32)
                 total = own + pair_in[q, yy, xx].astype(F32)
-                pair_sum[q, xx + core * (yy - xx), yy + core * (xx - yy)] = total.astype(BF)
+                pair_sum[q, xx + turns[q] * (yy - xx), yy + turns[q] * (xx - yy)] = total.astype(BF)
         for d in range(1, 4):
-            there, device = first_peer(d)
+            there, device = first_peer(q, d)
             send(pair_sum.at[q, there], first_in.at[q, 3 - d], first_send.at[q], first_recv.at[q], device)
 
     def first_finish(q):
         group_wait(first_in.at[q], first_recv.at[q])
         for s in range(4):
-            total = pair_sum[q, my_first, s].astype(F32)
+            total = pair_sum[q, my_first[q], s].astype(F32)
             for d in range(3):
                 total = total + first_in[q, d, s].astype(F32)
             first_sum[q, s] = total.astype(BF)
         for d in range(1, 4):
-            there, device = second_peer(d)
+            there, device = second_peer(q, d)
             send(first_sum.at[q, there], second_in.at[q, 3 - d], second_send.at[q], second_recv.at[q], device)
 
     def second_finish(q):
         group_wait(second_in.at[q], second_recv.at[q])
-        total = first_sum[q, my_second].astype(F32)
+        total = first_sum[q, my_second[q]].astype(F32)
         for d in range(3):
             total = total + second_in[q, d].astype(F32)
         second_sum[q] = total.astype(BF)
@@ -468,6 +467,17 @@
     @pl.when(at_end)
     def _():
         group_wait(z_in, out_send)
+
+
+def store_kernel(grad_input_ref, share_ref, grad_input_out, share_out, sem):
+    copies = [
+        pltpu.make_async_copy(grad_input_ref, grad_input_out, sem.at[0]),
+        pltpu.make_async_copy(share_ref, share_out, sem.at[1]),
+    ]
+    for copy in copies:
+        copy.start()
+    for copy in copies:
+        copy.wait()
 
 
 def per_device(inputs, cotangent, w_conv, w_down, w_up):
@@ -520,6 +530,18 @@
         ),
         name="whole_step",
     )(inputs.reshape(8, 64, 128), cotangent.reshape(8, 64, 128), w_conv, w_down, w_up)
+    grad_input, share = pl.pallas_call(
+        store_kernel,
+        out_shape=(
+            jax.ShapeDtypeStruct((8, 64, 128), BF),
+            jax.ShapeDtypeStruct((SHARE, 128), F32),
+        ),
+        in_specs=[pl.BlockSpec(memory_space=pl.ANY)] * 2,
+        out_specs=(pl.BlockSpec(memory_space=pl.ANY),) * 2,
+        scratch_shapes=[dma((2,))],
+        compiler_params=pltpu.CompilerParams(vmem_limit_bytes=1024 * 1024),
+        name="store",
+    )(grad_input, share)
     return (grad_input.reshape(inputs.shape), share.reshape(-1))
 
 

time: 48.8 us -> 47.4 us (0.971)
  local copies, waits for them, and re-layouts: 1.29 us -> 0 us
    unnamed x2 -> x0, local copies, waits for them, and re-layouts: 1.29 us -> none
    pallas_call x1, Pallas kernels: 46.8 us -> 46 us  [per_device(): pl.pallas_call(kernel, out_shape=(jax.ShapeDtypeStruct((8, 64, 128), BF),...]
    pallas_call x0 -> x1, Pallas kernels: none -> 0.69 us  [per_device(): pl.pallas_call(store_kernel, out_shape=(jax.ShapeDtypeStruct((8, 64, 128)...]
where the time goes in v5:
time: 47.4 us; the launch traced here: 47.3 us
  Pallas kernels  46.7 us (99%)
  between operations  0.64 us (1%)
    pallas_call x1, Pallas kernels, per_device(): pl.pallas_call(kernel, out_shape=(jax.ShapeDtypeStruct((8, 64, 128), BF),...  46 us

profile of v5, /device:TPU:1, one launch (start us, length us, event | category | flops | bytes accessed | tf_op | source)
XLA Modules:
  0.0 47.3 jit_solution(11350217511866242886)
XLA Ops:
  0.6 46.0 %whole_step.1 = (bf16[8,64,128]{2,1,0:T(8,128)(2,1)S(1)}, f32[118,128]{1,0:T(8,128)S(1)}) custom-call(bf16[8,64,128]{2,1,0:T(8,128)(2,1)} %bitcast.6, bf16[8,64,128]{2,1,0:T(8,128)(2,1)} %bitcast.7, bf16[3456,128]{1,0:T(8,128)(2,1)} %refs_2_.1, bf16[1024,256]{1,0:T(8,128)(2,1)} %refs_3_.1, bf16[2048,128]{1,0:T(8,128)(2,1)} %refs_4_.1), custom_call_target="tpu_custom_call" | custom-call | tf_op jit(solution)/shard_map/whole_step/pallas_call | solution.py:493
  46.6 0.7 %store.1 = (bf16[8,64,128]{2,1,0:T(8,128)(2,1)}, f32[118,128]{1,0:T(8,128)}) custom-call(bf16[8,64,128]{2,1,0:T(8,128)(2,1)S(1)} %get-tuple-element.6.grad_input_ref, f32[118,128]{1,0:T(8,128)S(1)} %get-tuple-element.7.share_ref), custom_call_target="tpu_custom_call" | custom-call | tf_op jit(solution)/shard_map/store/pallas_call | solution.py:533

commit v6 on v5

--- a/solution.py
+++ b/solution.py
@@ -172,14 +172,111 @@
     pltpu.make_async_copy(ref, ref, sem).wait()
 
 
+def remote(src, dst, send_sem, recv_sem, device):
+    pltpu.make_async_remote_copy(
+        src_ref=src, dst_ref=dst, send_sem=send_sem, recv_sem=recv_sem, device_id=device, device_id_type=MESH
+    ).start()
+
+
+def planes_kernel(
+    inputs_ref, cotangent_ref, w_conv_any, field, upstream, w_conv,
+    load_sem, near_send, near_recv, low_recv, high_recv,
+):
+    sp = lax.axis_index("sp")
+    dp = lax.axis_index("dp")
+    core = lax.rem(sp, 2)
+    z_lo = lax.div(sp, 2)
+    below = lax.div(z_lo + 3, 4)
+    above = 1 - lax.div(z_lo, 3)
+    sibling = {"sp": sp + 1 - 2 * core, "dp": dp}
+    barrier = pltpu.get_barrier_semaphore()
+
+    def greet(there):
+        pl.semaphore_signal(barrier, inc=1, device_id={"sp": there, "dp": dp}, device_id_type=MESH)
+
+    @pl.when(z_lo > 0)
+    def _():
+        greet(2 * z_lo - 1)
+
+        @pl.when(core == 0)
+        def _():
+            greet(sp - 2)
+
+    @pl.when(z_lo < 3)
+    def _():
+        greet(2 * z_lo + 2)
+
+        @pl.when(core == 1)
+        def _():
+            greet(sp + 2)
+
+    greet(sp + 1 - 2 * core)
+    own_crops = pl.ds(4 * core, 4)
+    far_crops = pl.ds(4 * (1 - core), 4)
+    loads = [
+        pltpu.make_async_copy(inputs_ref.at[own_crops], field.at[1 + core], load_sem.at[0]),
+        pltpu.make_async_copy(cotangent_ref.at[own_crops], upstream.at[core], load_sem.at[1]),
+        pltpu.make_async_copy(w_conv_any, w_conv, load_sem.at[2]),
+    ]
+    for load in loads:
+        load.start()
+    pl.semaphore_wait(barrier, 1 + below * (2 - core) + above * (1 + core))
+
+    @pl.when(core == 0)
+    def _():
+        @pl.when(z_lo > 0)
+        def _():
+            for c in range(2):
+                remote(inputs_ref.at[pl.ds(4 * c, 4)], field.at[3], near_send.at[1 + c], high_recv, {"sp": sp - 2 + c, "dp": dp})
+
+    @pl.when(core == 1)
+    def _():
+        @pl.when(z_lo < 3)
+        def _():
+            for c in range(2):
+                remote(inputs_ref.at[pl.ds(4 * c, 4)], field.at[0], near_send.at[1 + c], low_recv, {"sp": sp + 1 + c, "dp": dp})
+
+    remote(inputs_ref.at[far_crops], field.at[1 + core], near_send.at[0], near_recv.at[0], sibling)
+    remote(cotangent_ref.at[far_crops], upstream.at[core], near_send.at[3], near_recv.at[1], sibling)
+
+    @pl.when(z_lo == 0)
+    def _():
+        field[0] = jnp.zeros((4, 64, 128), BF)
+
+    @pl.when(z_lo == 3)
+    def _():
+        field[3] = jnp.zeros((4, 64, 128), BF)
+
+    for load in loads:
+        load.wait()
+    group_wait(field.at[0], near_recv.at[0])
+    group_wait(field.at[0], near_recv.at[1])
+    group_wait(field.at[0], near_send.at[0])
+    group_wait(field.at[0], near_send.at[3])
+    side = z_lo - 1 + 2 * core
+
+    @pl.when(jnp.logical_and(side >= 0, side <= 3))
+    def _():
+        group_wait(field.at[0], near_send.at[1])
+        group_wait(field.at[0], near_send.at[2])
+
+    @pl.when(z_lo > 0)
+    def _():
+        group_wait(field.at[0], low_recv)
+
+    @pl.when(z_lo < 3)
+    def _():
+        group_wait(field.at[3], high_recv)
+
+
 def step_kernel(
     scale,
-    inputs_ref, cotangent_ref, w_conv_any, w_down_any, w_up_any,
+    field, upstream, w_conv, w_down, w_up,
     grad_input_ref, share_ref,
-    field, upstream, w_conv, w_down, w_up, w_flip, columns, turned, slope, order, back, twice, rows,
+    w_flip, columns, turned, slope, order, back, twice, rows,
     grad_field, grad_out,
     pair_in, pair_sum, first_in, first_sum, second_in, second_sum, z_in, final,
-    load_sem, own_sem, near_send, near_recv, low_recv, high_recv, halo_send, halo_low, halo_high, grad_send, grad_recv,
+    own_sem, halo_send, halo_low, halo_high, grad_send, grad_recv,
     pair_send, pair_recv, first_send, first_recv, second_send, second_recv, z_send, z_recv, out_send, out_recv,
 ):
     sp = lax.axis_index("sp")
@@ -211,11 +308,6 @@
     def greet(device):
         pl.semaphore_signal(barrier, inc=1, device_id=device, device_id_type=MESH)
 
-    def send(src, dst, send_sem, recv_sem, device):
-        pltpu.make_async_remote_copy(
-            src_ref=src, dst_ref=dst, send_sem=send_sem, recv_sem=recv_sem, device_id=device, device_id_type=MESH
-        ).start()
-
     at_end = jnp.logical_or(z_lo == 0, z_lo == 3)
 
     def along_z(offset):
@@ -234,49 +326,7 @@
         greet(second_peer(0, d)[1])
 
     own_crops = pl.ds(4 * core, 4)
-    far_crops = pl.ds(4 * (1 - core), 4)
     sibling = {"sp": sp + 1 - 2 * core, "dp": dp}
-    side = z_lo - 1 + 2 * core
-    has_side = jnp.logical_and(side >= 0, side <= 3)
-    loads = [
-        pltpu.make_async_copy(inputs_ref.at[own_crops], field.at[1 + core], own_sem.at[0]),
-        pltpu.make_async_copy(cotangent_ref.at[own_crops], upstream.at[core], own_sem.at[1]),
-        pltpu.make_async_copy(w_conv_any, w_conv, load_sem.at[0]),
-        pltpu.make_async_copy(w_down_any, w_down, load_sem.at[1]),
-        pltpu.make_async_copy(w_up_any, w_up, load_sem.at[2]),
-    ]
-    for load in loads:
-        load.start()
-
-    @pl.when(z_lo == 0)
-    def _():
-        field[0] = jnp.zeros((4, 64, 128), BF)
-        grad_field[0] = jnp.zeros((4, 64, 128), BF)
-
-    @pl.when(z_lo == 3)
-    def _():
-        field[3] = jnp.zeros((4, 64, 128), BF)
-        grad_field[3] = jnp.zeros((4, 64, 128), BF)
-
-    pl.semaphore_wait(barrier, 16 + 2 * (z_lo - 1) * (z_lo - 2))
-
-    @pl.when(core == 0)
-    def _():
-        @pl.when(z_lo > 0)
-        def _():
-            for c in range(2):
-                send(inputs_ref.at[pl.ds(4 * c, 4)], field.at[3], near_send.at[1 + c], high_recv, {"sp": sp - 2 + c, "dp": dp})
-
-    @pl.when(core == 1)
-    def _():
-        @pl.when(z_lo < 3)
-        def _():
-            for c in range(2):
-                send(inputs_ref.at[pl.ds(4 * c, 4)], field.at[0], near_send.at[1 + c], low_recv, {"sp": sp + 1 + c, "dp": dp})
-
-    send(inputs_ref.at[far_crops], field.at[1 + core], near_send.at[0], near_recv.at[0], sibling)
-    send(cotangent_ref.at[far_crops], upstream.at[core], near_send.at[3], near_recv.at[1], sibling)
-
     def goes_low(place):
         return jnp.logical_or(place == 1, place >= 10)
 
@@ -286,7 +336,7 @@
     def pair_start(q):
         for xx in range(4):
             src = rows.at[pl.ds(4 * q, 4), pl.ds(STARTS[xx] + 8 * (1 - core), 8)]
-            send(src, pair_in.at[q, :, xx], pair_send.at[q], pair_recv.at[q], sibling)
+            remote(src, pair_in.at[q, :, xx], pair_send.at[q], pair_recv.at[q], sibling)
 
     def pair_finish(q):
         group_wait(pair_in.at[q], pair_recv.at[q])
@@ -297,7 +347,7 @@
                 pair_sum[q, xx + turns[q] * (yy - xx), yy + turns[q] * (xx - yy)] = total.astype(BF)
         for d in range(1, 4):
             there, device = first_peer(q, d)
-            send(pair_sum.at[q, there], first_in.at[q, 3 - d], first_send.at[q], first_recv.at[q], device)
+            remote(pair_sum.at[q, there], first_in.at[q, 3 - d], first_send.at[q], first_recv.at[q], device)
 
     def first_finish(q):
         group_wait(first_in.at[q], first_recv.at[q])
@@ -308,7 +358,7 @@
             first_sum[q, s] = total.astype(BF)
         for d in range(1, 4):
             there, device = second_peer(q, d)
-            send(first_sum.at[q, there], second_in.at[q, 3 - d], second_send.at[q], second_recv.at[q], device)
+            remote(first_sum.at[q, there], second_in.at[q, 3 - d], second_send.at[q], second_recv.at[q], device)
 
     def second_finish(q):
         group_wait(second_in.at[q], second_recv.at[q])
@@ -322,74 +372,56 @@
         @pl.when(goes_low(place))
         def _():
             slot = lax.rem(place + 7, 8) * lax.div(place, 10)
-            send(second_sum.at[q], z_in.at[slot], z_send.at[q], z_recv, {"sp": core, "dp": there})
+            remote(second_sum.at[q], z_in.at[slot], z_send.at[q], z_recv, {"sp": core, "dp": there})
 
         @pl.when(goes_high(place))
         def _():
             slot = (place - 3) * lax.div(place + 12, 16)
-            send(second_sum.at[q], z_in.at[slot], z_send.at[q], z_recv, {"sp": 6 + core, "dp": there})
+            remote(second_sum.at[q], z_in.at[slot], z_send.at[q], z_recv, {"sp": 6 + core, "dp": there})
+
+    @pl.when(z_lo == 0)
+    def _():
+        grad_field[0] = jnp.zeros((4, 64, 128), BF)
+
+    @pl.when(z_lo == 3)
+    def _():
+        grad_field[3] = jnp.zeros((4, 64, 128), BF)
 
     order_matrices(order, back, twice)
-    loads[2].wait()
-    flip_weights(w_conv, w_flip)
-
-    loads[0].wait()
-    group_wait(field.at[0], near_recv.at[0])
-    fill_plane(columns, field, 1, 2)
-    pre_conv = tap_dot(columns, w_conv, 1)
-    turned[:, 256:768] = columns[256:768, :].T
-
-    @pl.when(z_lo > 0)
-    def _():
-        group_wait(field.at[0], low_recv)
-
-    @pl.when(z_lo < 3)
-    def _():
-        group_wait(field.at[3], high_recv)
-
-    fill_plane(columns, field, 0)
-    fill_plane(columns, field, 3)
-    pre_conv += tap_dot(columns, w_conv, 0)
+    fill_plane(columns, field, 0, 4)
+    pre_conv = tap_dot(columns, w_conv, 0)
+    pre_conv += tap_dot(columns, w_conv, 1)
     pre_conv += tap_dot(columns, w_conv, 2)
     hidden, pre_slope = logistic_parts(pre_conv)
     slope[...] = pre_slope
     hid_taps = to_blocks(order[...], hidden.astype(BF))
-    loads[3].wait()
     deep_act, deep_slope = deep_forward(hid_taps, w_down)
-
-    loads[1].wait()
-    group_wait(upstream.at[0], near_recv.at[1])
+    turned[...] = columns[...].T
     up_taps = to_blocks(order[...], upstream[...].reshape(512, 128))
+    grad_deep = deep_grads(up_taps, deep_slope, w_up)
     up_grads(rows, deep_act, up_taps)
-    pair_start(3)
-    loads[4].wait()
-    grad_deep = deep_grads(up_taps, deep_slope, w_up)
-    down_grads(rows, hid_taps, twice[...], grad_deep)
-    pair_start(2)
     grad_pre = pre_grads(upstream, grad_deep, w_down, back[...], slope).astype(BF)
     grad_field[1:3] = grad_pre.reshape(2, 4, 64, 128)
+    down_grads(rows, hid_taps, twice[...], grad_deep)
+    for i in (2, 1, 0):
+        conv_grads(rows, turned, grad_pre, i)
+    flip_weights(w_conv, w_flip)
+
+    pl.semaphore_wait(barrier, 16 + 2 * (z_lo - 1) * (z_lo - 2))
+    for q in (3, 2, 1, 0):
+        pair_start(q)
 
     @pl.when(z_lo > 0)
     def _():
-        send(grad_field.at[1], grad_field.at[3], halo_send.at[0], halo_high, {"sp": sp - 2, "dp": dp})
+        remote(grad_field.at[1], grad_field.at[3], halo_send.at[0], halo_high, {"sp": sp - 2, "dp": dp})
 
     @pl.when(z_lo < 3)
     def _():
-        send(grad_field.at[2], grad_field.at[0], halo_send.at[1], halo_low, {"sp": sp + 2, "dp": dp})
-
-    turned[:, 0:256] = columns[0:256, :].T
-    turned[:, 768:1024] = columns[768:1024, :].T
-    conv_grads(rows, turned, grad_pre, 2)
-    conv_grads(rows, turned, grad_pre, 1)
-    pair_start(1)
-    pair_finish(3)
-    conv_grads(rows, turned, grad_pre, 0)
-    pair_start(0)
-
-    pair_finish(2)
+        remote(grad_field.at[2], grad_field.at[0], halo_send.at[1], halo_low, {"sp": sp + 2, "dp": dp})
+
+    for q in (3, 2, 1, 0):
+        pair_finish(q)
     fill_plane(columns, grad_field, 1, 2)
-    pair_finish(1)
-    pair_finish(0)
 
     @pl.when(z_lo > 0)
     def _():
@@ -407,8 +439,8 @@
     grad_out[...] = total.astype(BF).reshape(2, 4, 64, 128)
     for q in (3, 2, 1, 0):
         first_finish(q)
-    send(grad_out.at[1 - core], grad_input_ref.at[own_crops], grad_send, grad_recv, sibling)
-    own_grad = pltpu.make_async_copy(grad_out.at[core], grad_input_ref.at[own_crops], own_sem.at[2])
+    remote(grad_out.at[1 - core], grad_input_ref.at[own_crops], grad_send, grad_recv, sibling)
+    own_grad = pltpu.make_async_copy(grad_out.at[core], grad_input_ref.at[own_crops], own_sem)
     own_grad.start()
     for q in (3, 2, 1, 0):
         second_finish(q)
@@ -422,7 +454,7 @@
         end = lax.div(z_lo, 3)
         final[end, core] = total.astype(BF)
         for d in range(1, 8):
-            send(final.at[end, core], final.at[end, core], out_send, out_recv, member(d)[1])
+            remote(final.at[end, core], final.at[end, core], out_send, out_recv, member(d)[1])
         group_wait(z_in.at[pl.ds(0, 3)], out_recv)
 
     @pl.when(jnp.logical_not(at_end))
@@ -438,14 +470,6 @@
     own_grad.wait()
     group_wait(grad_out.at[0], grad_recv)
     group_wait(grad_out.at[0], grad_send)
-    group_wait(field.at[0], near_send.at[0])
-    group_wait(field.at[0], near_send.at[3])
-
-    @pl.when(has_side)
-    def _():
-        group_wait(field.at[0], near_send.at[1])
-        group_wait(field.at[0], near_send.at[2])
-
     @pl.when(z_lo > 0)
     def _():
         group_wait(grad_field.at[0], halo_send.at[0])
@@ -490,20 +514,34 @@
 
     dma = pltpu.SemaphoreType.DMA
     vmem = pltpu.VMEM
+    field, upstream, w_conv = pl.pallas_call(
+        planes_kernel,
+        out_shape=(
+            jax.ShapeDtypeStruct((4, 4, 64, 128), BF),
+            jax.ShapeDtypeStruct((2, 4, 64, 128), BF),
+            jax.ShapeDtypeStruct((3456, 128), BF),
+        ),
+        in_specs=[pl.BlockSpec(memory_space=pl.ANY)] * 3,
+        out_specs=(pl.BlockSpec(memory_space=vmem),) * 3,
+        scratch_shapes=[dma((3,)), dma((4,)), dma((2,)), dma, dma],
+        compiler_params=pltpu.CompilerParams(
+            collective_id=0, has_side_effects=True, vmem_limit_bytes=16 * 1024 * 1024
+        ),
+        name="planes",
+    )(
+        pltpu.with_memory_space_constraint(inputs.reshape(8, 64, 128), pltpu.HBM),
+        pltpu.with_memory_space_constraint(cotangent.reshape(8, 64, 128), pltpu.HBM),
+        pltpu.with_memory_space_constraint(w_conv, pltpu.HBM),
+    )
     grad_input, share = pl.pallas_call(
         kernel,
         out_shape=(
             jax.ShapeDtypeStruct((8, 64, 128), BF),
             jax.ShapeDtypeStruct((SHARE, 128), F32),
         ),
-        in_specs=[pl.BlockSpec(memory_space=pl.ANY)] * 5,
+        in_specs=[pl.BlockSpec(memory_space=vmem)] * 5,
         out_specs=(pl.BlockSpec(memory_space=vmem), pl.BlockSpec(memory_space=vmem)),
         scratch_shapes=[
-            vmem((4, 4, 64, 128), BF),
-            vmem((2, 4, 64, 128), BF),
-            vmem((3456, 128), BF),
-            vmem((1024, 256), BF),
-            vmem((2048, 128), BF),
             vmem((3456, 128), BF),
             vmem((1024, 1152), BF),
             vmem((1152, 1024), BF),
@@ -522,14 +560,14 @@
             vmem((4, 8, 8, 128), BF),
             vmem((7, 8, 8, 128), BF),
             vmem((2, 2, 8, 8, 128), BF),
-            dma((3,)), dma((3,)), dma((4,)), dma((2,)), dma, dma, dma((2,)), dma, dma, dma, dma,
+            dma, dma((2,)), dma, dma, dma, dma,
             dma((4,)), dma((4,)), dma((4,)), dma((4,)), dma((4,)), dma((4,)), dma((4,)), dma, dma, dma,
         ],
         compiler_params=pltpu.CompilerParams(
-            collective_id=0, has_side_effects=True, vmem_limit_bytes=55040 * 1024
+            collective_id=1, has_side_effects=True, vmem_limit_bytes=48 * 1024 * 1024
         ),
         name="whole_step",
-    )(inputs.reshape(8, 64, 128), cotangent.reshape(8, 64, 128), w_conv, w_down, w_up)
+    )(field, upstream, w_conv, w_down, w_up)
     grad_input, share = pl.pallas_call(
         store_kernel,
         out_shape=(

time: 47.4 us -> 49 us (1.034)
  Pallas kernels: 46.7 us -> 48.2 us
    pallas_call x0 -> x1, Pallas kernels: none -> 12.3 us  [per_device(): pl.pallas_call(planes_kernel, out_shape=(jax.ShapeDtypeStruct((4, 4, 64,...]
    pallas_call x1, Pallas kernels: 46 us -> 35.2 us  [per_device(): pl.pallas_call(kernel, out_shape=(jax.ShapeDtypeStruct((8, 64, 128), BF),...]
where the time goes in v6:
time: 49 us; the launch traced here: 48.9 us
  Pallas kernels  48.2 us (98%)
  between operations  0.68 us (1%)
    pallas_call x1, Pallas kernels, per_device(): pl.pallas_call(kernel, out_shape=(jax.ShapeDtypeStruct((8, 64, 128), BF),...  35.2 us
    pallas_call x1, Pallas kernels, per_device(): pl.pallas_call(planes_kernel, out_shape=(jax.ShapeDtypeStruct((4, 4, 64,...  12.3 us

profile of v6, /device:TPU:1, one launch (start us, length us, event | category | flops | bytes accessed | tf_op | source)
XLA Modules:
  0.0 48.9 jit_solution(13969781177336043264)
XLA Ops:
  0.6 0.0 copy-start
  0.6 0.0 copy-start.1
  0.7 12.3 %planes.1 = (bf16[4,4,64,128]{3,2,1,0:T(8,128)(2,1)S(1)}, bf16[2,4,64,128]{3,2,1,0:T(8,128)(2,1)S(1)}, bf16[3456,128]{1,0:T(8,128)(2,1)S(1)}) custom-call(bf16[8,64,128]{2,1,0:T(8,128)(2,1)} %bitcast.6, bf16[8,64,128]{2,1,0:T(8,128)(2,1)} %bitcast.7, bf16[3456,128]{1,0:T(8,128)(2,1)} %w_conv_any.1), custom_call_target="tpu_custom_call" | custom-call | tf_op jit(solution)/shard_map/planes/pallas_call | solution.py:517
  13.0 0.0 copy-done
  13.0 0.0 copy-done.1
  13.0 35.2 %whole_step.1 = (bf16[8,64,128]{2,1,0:T(8,128)(2,1)S(1)}, f32[118,128]{1,0:T(8,128)S(1)}) custom-call(bf16[4,4,64,128]{3,2,1,0:T(8,128)(2,1)S(1)} %get-tuple-element.9.refs_0_, bf16[2,4,64,128]{3,2,1,0:T(8,128)(2,1)S(1)} %get-tuple-element.10.refs_1_, bf16[3456,128]{1,0:T(8,128)(2,1)S(1)} %get-tuple-element.11.refs_2_, bf16[1024,256]{1,0:T(8,128)(2,1)S(1)} %copy-done, ...), custom_call_target="tpu_custom_call" | custom-call | tf_op jit(solution)/shard_map/whole_step/pallas_call | solution.py:536
  48.2 0.7 %store.1 = (bf16[8,64,128]{2,1,0:T(8,128)(2,1)}, f32[118,128]{1,0:T(8,128)}) custom-call(bf16[8,64,128]{2,1,0:T(8,128)(2,1)S(1)} %get-tuple-element.12.grad_input_ref, f32[118,128]{1,0:T(8,128)S(1)} %get-tuple-element.13.share_ref), custom_call_target="tpu_custom_call" | custom-call | tf_op jit(solution)/shard_map/store/pallas_call | solution.py:571
Async XLA Ops:
  0.6 12.3 %copy-start = (bf16[1024,256]{1,0:T(8,128)(2,1)S(1)}, bf16[1024,256]{1,0:T(8,128)(2,1)}, u32[]{:S(2)}) copy-start(bf16[1024,256]{1,0:T(8,128)(2,1)} %refs_3_.1) | copy-start | bytes 1572868
  0.6 12.3 %copy-start.1 = (bf16[2048,128]{1,0:T(8,128)(2,1)S(1)}, bf16[2048,128]{1,0:T(8,128)(2,1)}, u32[]{:S(2)}) copy-start(bf16[2048,128]{1,0:T(8,128)(2,1)} %refs_4_.1) | copy-start | bytes 1572868

commit v7 on v6

--- a/solution.py
+++ b/solution.py
@@ -345,7 +345,7 @@
                 own = rows[4 * q + yy, pl.ds(STARTS[xx] + 8 * core, 8)].astype(F32)
                 total = own + pair_in[q, yy, xx].astype(F32)
                 pair_sum[q, xx + turns[q] * (yy - xx), yy + turns[q] * (xx - yy)] = total.astype(BF)
-        for d in range(1, 4):
+        for d in (2, 1, 3):
             there, device = first_peer(q, d)
             remote(pair_sum.at[q, there], first_in.at[q, 3 - d], first_send.at[q], first_recv.at[q], device)
 
@@ -356,7 +356,7 @@
             for d in range(3):
                 total = total + first_in[q, d, s].astype(F32)
             first_sum[q, s] = total.astype(BF)
-        for d in range(1, 4):
+        for d in (2, 1, 3):
             there, device = second_peer(q, d)
             remote(first_sum.at[q, there], second_in.at[q, 3 - d], second_send.at[q], second_recv.at[q], device)
 
@@ -399,28 +399,31 @@
     turned[...] = columns[...].T
     up_taps = to_blocks(order[...], upstream[...].reshape(512, 128))
     grad_deep = deep_grads(up_taps, deep_slope, w_up)
-    up_grads(rows, deep_act, up_taps)
     grad_pre = pre_grads(upstream, grad_deep, w_down, back[...], slope).astype(BF)
     grad_field[1:3] = grad_pre.reshape(2, 4, 64, 128)
+    for i in (0, 1):
+        conv_grads(rows, turned, grad_pre, i)
+
+    pl.semaphore_wait(barrier, 16 + 2 * (z_lo - 1) * (z_lo - 2))
+    pair_start(0)
+    conv_grads(rows, turned, grad_pre, 2)
     down_grads(rows, hid_taps, twice[...], grad_deep)
-    for i in (2, 1, 0):
-        conv_grads(rows, turned, grad_pre, i)
+    pair_start(1)
+    up_grads(rows, deep_act, up_taps)
+    pair_start(2)
+    pair_start(3)
+
+    @pl.when(z_lo > 0)
+    def _():
+        remote(grad_field.at[1], grad_field.at[3], halo_send.at[0], halo_high, {"sp": sp - 2, "dp": dp})
+
+    @pl.when(z_lo < 3)
+    def _():
+        remote(grad_field.at[2], grad_field.at[0], halo_send.at[1], halo_low, {"sp": sp + 2, "dp": dp})
+
+    pair_finish(0)
+    pair_finish(1)
     flip_weights(w_conv, w_flip)
-
-    pl.semaphore_wait(barrier, 16 + 2 * (z_lo - 1) * (z_lo - 2))
-    for q in (3, 2, 1, 0):
-        pair_start(q)
-
-    @pl.when(z_lo > 0)
-    def _():
-        remote(grad_field.at[1], grad_field.at[3], halo_send.at[0], halo_high, {"sp": sp - 2, "dp": dp})
-
-    @pl.when(z_lo < 3)
-    def _():
-        remote(grad_field.at[2], grad_field.at[0], halo_send.at[1], halo_low, {"sp": sp + 2, "dp": dp})
-
-    for q in (3, 2, 1, 0):
-        pair_finish(q)
     fill_plane(columns, grad_field, 1, 2)
 
     @pl.when(z_lo > 0)
@@ -437,13 +440,19 @@
     total += tap_dot(columns, w_flip, 1)
     total += tap_dot(columns, w_flip, 2)
     grad_out[...] = total.astype(BF).reshape(2, 4, 64, 128)
-    for q in (3, 2, 1, 0):
-        first_finish(q)
+    first_finish(0)
+    pair_finish(2)
+    first_finish(1)
+    pair_finish(3)
     remote(grad_out.at[1 - core], grad_input_ref.at[own_crops], grad_send, grad_recv, sibling)
     own_grad = pltpu.make_async_copy(grad_out.at[core], grad_input_ref.at[own_crops], own_sem)
     own_grad.start()
-    for q in (3, 2, 1, 0):
-        second_finish(q)
+    second_finish(0)
+    first_finish(2)
+    second_finish(1)
+    first_finish(3)
+    second_finish(2)
+    second_finish(3)
 
     @pl.when(at_end)
     def _():
@@ -453,8 +462,11 @@
             total = total + z_in[d].astype(F32)
         end = lax.div(z_lo, 3)
         final[end, core] = total.astype(BF)
-        for d in range(1, 8):
-            remote(final.at[end, core], final.at[end, core], out_send, out_recv, member(d)[1])
+        for step in range(3):
+            for c in range(2):
+                there = 2 * (3 - step - end * (3 - 2 * step)) + c
+                remote(final.at[end, core], final.at[end, core], out_send, out_recv, {"sp": there, "dp": dp})
+        remote(final.at[end, core], final.at[end, core], out_send, out_recv, sibling)
         group_wait(z_in.at[pl.ds(0, 3)], out_recv)
 
     @pl.when(jnp.logical_not(at_end))

time: 49 us -> 45.2 us (0.922)
  Pallas kernels: 48.2 us -> 44.4 us
    pallas_call x1, Pallas kernels: 35.2 us -> 31.4 us  [per_device(): pl.pallas_call(kernel, out_shape=(jax.ShapeDtypeStruct((8, 64, 128), BF),...]
where the time goes in v7:
time: 45.2 us; the launch traced here: 45.1 us
  Pallas kernels  44.4 us (98%)
  between operations  0.68 us (2%)
    pallas_call x1, Pallas kernels, per_device(): pl.pallas_call(kernel, out_shape=(jax.ShapeDtypeStruct((8, 64, 128), BF),...  31.4 us
    pallas_call x1, Pallas kernels, per_device(): pl.pallas_call(planes_kernel, out_shape=(jax.ShapeDtypeStruct((4, 4, 64,...  12.3 us

profile of v7, /device:TPU:1, one launch (start us, length us, event | category | flops | bytes accessed | tf_op | source)
XLA Modules:
  0.0 45.1 jit_solution(4504392622711115876)
XLA Ops:
  0.6 0.0 copy-start
  0.6 0.0 copy-start.1
  0.7 12.3 %planes.1 = (bf16[4,4,64,128]{3,2,1,0:T(8,128)(2,1)S(1)}, bf16[2,4,64,128]{3,2,1,0:T(8,128)(2,1)S(1)}, bf16[3456,128]{1,0:T(8,128)(2,1)S(1)}) custom-call(bf16[8,64,128]{2,1,0:T(8,128)(2,1)} %bitcast.6, bf16[8,64,128]{2,1,0:T(8,128)(2,1)} %bitcast.7, bf16[3456,128]{1,0:T(8,128)(2,1)} %w_conv_any.1), custom_call_target="tpu_custom_call" | custom-call | tf_op jit(solution)/shard_map/planes/pallas_call | solution.py:529
  13.0 0.0 copy-done
  13.0 0.0 copy-done.1
  13.0 31.4 %whole_step.1 = (bf16[8,64,128]{2,1,0:T(8,128)(2,1)S(1)}, f32[118,128]{1,0:T(8,128)S(1)}) custom-call(bf16[4,4,64,128]{3,2,1,0:T(8,128)(2,1)S(1)} %get-tuple-element.9.refs_0_, bf16[2,4,64,128]{3,2,1,0:T(8,128)(2,1)S(1)} %get-tuple-element.10.refs_1_, bf16[3456,128]{1,0:T(8,128)(2,1)S(1)} %get-tuple-element.11.refs_2_, bf16[1024,256]{1,0:T(8,128)(2,1)S(1)} %copy-done, ...), custom_call_target="tpu_custom_call" | custom-call | tf_op jit(solution)/shard_map/whole_step/pallas_call | solution.py:548
  44.4 0.7 %store.1 = (bf16[8,64,128]{2,1,0:T(8,128)(2,1)}, f32[118,128]{1,0:T(8,128)}) custom-call(bf16[8,64,128]{2,1,0:T(8,128)(2,1)S(1)} %get-tuple-element.12.grad_input_ref, f32[118,128]{1,0:T(8,128)S(1)} %get-tuple-element.13.share_ref), custom_call_target="tpu_custom_call" | custom-call | tf_op jit(solution)/shard_map/store/pallas_call | solution.py:583
Async XLA Ops:
  0.6 12.3 %copy-start = (bf16[1024,256]{1,0:T(8,128)(2,1)S(1)}, bf16[1024,256]{1,0:T(8,128)(2,1)}, u32[]{:S(2)}) copy-start(bf16[1024,256]{1,0:T(8,128)(2,1)} %refs_3_.1) | copy-start | bytes 1572868
  0.6 12.3 %copy-start.1 = (bf16[2048,128]{1,0:T(8,128)(2,1)S(1)}, bf16[2048,128]{1,0:T(8,128)(2,1)}, u32[]{:S(2)}) copy-start(bf16[2048,128]{1,0:T(8,128)(2,1)} %refs_4_.1) | copy-start | bytes 1572868

commit v8 on v7

--- a/solution.py
+++ b/solution.py
@@ -179,8 +179,8 @@
 
 
 def planes_kernel(
-    inputs_ref, cotangent_ref, w_conv_any, field, upstream, w_conv,
-    load_sem, near_send, near_recv, low_recv, high_recv,
+    inputs_ref, cotangent_ref, w_conv_any, w_down_any, w_up_any, columns, middle, upstream, w_conv, w_down, w_up,
+    field, load_sem, near_send, near_recv, low_recv, high_recv,
 ):
     sp = lax.axis_index("sp")
     dp = lax.axis_index("dp")
@@ -217,6 +217,8 @@
         pltpu.make_async_copy(inputs_ref.at[own_crops], field.at[1 + core], load_sem.at[0]),
         pltpu.make_async_copy(cotangent_ref.at[own_crops], upstream.at[core], load_sem.at[1]),
         pltpu.make_async_copy(w_conv_any, w_conv, load_sem.at[2]),
+        pltpu.make_async_copy(w_down_any, w_down, load_sem.at[3]),
+        pltpu.make_async_copy(w_up_any, w_up, load_sem.at[4]),
     ]
     for load in loads:
         load.start()
@@ -250,6 +252,8 @@
     for load in loads:
         load.wait()
     group_wait(field.at[0], near_recv.at[0])
+    fill_plane(columns, field, 1, 2)
+    middle[...] = tap_dot(columns, w_conv, 1)
     group_wait(field.at[0], near_recv.at[1])
     group_wait(field.at[0], near_send.at[0])
     group_wait(field.at[0], near_send.at[3])
@@ -268,10 +272,13 @@
     def _():
         group_wait(field.at[3], high_recv)
 
+    fill_plane(columns, field, 0)
+    fill_plane(columns, field, 3)
+
 
 def step_kernel(
     scale,
-    field, upstream, w_conv, w_down, w_up,
+    planes, middle, upstream, w_conv, w_down, w_up,
     grad_input_ref, share_ref,
     w_flip, columns, turned, slope, order, back, twice, rows,
     grad_field, grad_out,
@@ -388,15 +395,13 @@
         grad_field[3] = jnp.zeros((4, 64, 128), BF)
 
     order_matrices(order, back, twice)
-    fill_plane(columns, field, 0, 4)
-    pre_conv = tap_dot(columns, w_conv, 0)
-    pre_conv += tap_dot(columns, w_conv, 1)
-    pre_conv += tap_dot(columns, w_conv, 2)
+    pre_conv = middle[...] + tap_dot(planes, w_conv, 0)
+    pre_conv += tap_dot(planes, w_conv, 2)
     hidden, pre_slope = logistic_parts(pre_conv)
     slope[...] = pre_slope
     hid_taps = to_blocks(order[...], hidden.astype(BF))
     deep_act, deep_slope = deep_forward(hid_taps, w_down)
-    turned[...] = columns[...].T
+    turned[...] = planes[...].T
     up_taps = to_blocks(order[...], upstream[...].reshape(512, 128))
     grad_deep = deep_grads(up_taps, deep_slope, w_up)
     grad_pre = pre_grads(upstream, grad_deep, w_down, back[...], slope).astype(BF)
@@ -526,16 +531,19 @@
 
     dma = pltpu.SemaphoreType.DMA
     vmem = pltpu.VMEM
-    field, upstream, w_conv = pl.pallas_call(
+    planes, middle, upstream, w_conv, w_down, w_up = pl.pallas_call(
         planes_kernel,
         out_shape=(
-            jax.ShapeDtypeStruct((4, 4, 64, 128), BF),
+            jax.ShapeDtypeStruct((1024, 1152), BF),
+            jax.ShapeDtypeStruct((512, 128), F32),
             jax.ShapeDtypeStruct((2, 4, 64, 128), BF),
             jax.ShapeDtypeStruct((3456, 128), BF),
+            jax.ShapeDtypeStruct((1024, 256), BF),
+            jax.ShapeDtypeStruct((2048, 128), BF),
         ),
-        in_specs=[pl.BlockSpec(memory_space=pl.ANY)] * 3,
-        out_specs=(pl.BlockSpec(memory_space=vmem),) * 3,
-        scratch_shapes=[dma((3,)), dma((4,)), dma((2,)), dma, dma],
+        in_specs=[pl.BlockSpec(memory_space=pl.ANY)] * 5,
+        out_specs=(pl.BlockSpec(memory_space=vmem),) * 6,
+        scratch_shapes=[vmem((4, 4, 64, 128), BF), dma((5,)), dma((4,)), dma((2,)), dma, dma],
         compiler_params=pltpu.CompilerParams(
             collective_id=0, has_side_effects=True, vmem_limit_bytes=16 * 1024 * 1024
         ),
@@ -544,6 +552,8 @@
         pltpu.with_memory_space_constraint(inputs.reshape(8, 64, 128), pltpu.HBM),
         pltpu.with_memory_space_constraint(cotangent.reshape(8, 64, 128), pltpu.HBM),
         pltpu.with_memory_space_constraint(w_conv, pltpu.HBM),
+        pltpu.with_memory_space_constraint(w_down, pltpu.HBM),
+        pltpu.with_memory_space_constraint(w_up, pltpu.HBM),
     )
     grad_input, share = pl.pallas_call(
         kernel,
@@ -551,7 +561,7 @@
             jax.ShapeDtypeStruct((8, 64, 128), BF),
             jax.ShapeDtypeStruct((SHARE, 128), F32),
         ),
-        in_specs=[pl.BlockSpec(memory_space=vmem)] * 5,
+        in_specs=[pl.BlockSpec(memory_space=vmem)] * 6,
         out_specs=(pl.BlockSpec(memory_space=vmem), pl.BlockSpec(memory_space=vmem)),
         scratch_shapes=[
             vmem((3456, 128), BF),
@@ -579,7 +589,7 @@
             collective_id=1, has_side_effects=True, vmem_limit_bytes=48 * 1024 * 1024
         ),
         name="whole_step",
-    )(field, upstream, w_conv, w_down, w_up)
+    )(planes, middle, upstream, w_conv, w_down, w_up)
     grad_input, share = pl.pallas_call(
         store_kernel,
         out_shape=(

time: 45.2 us -> 44.7 us (0.989)
  Pallas kernels: 44.4 us -> 43.9 us
    pallas_call x1, Pallas kernels: 31.4 us -> 30.8 us  [per_device(): pl.pallas_call(kernel, out_shape=(jax.ShapeDtypeStruct((8, 64, 128), BF),...]
where the time goes in v8:
time: 44.7 us; the launch traced here: 44.5 us
  Pallas kernels  43.9 us (98%)
  between operations  0.65 us (1%)
    pallas_call x1, Pallas kernels, per_device(): pl.pallas_call(kernel, out_shape=(jax.ShapeDtypeStruct((8, 64, 128), BF),...  30.8 us
    pallas_call x1, Pallas kernels, per_device(): pl.pallas_call(planes_kernel, out_shape=(jax.ShapeDtypeStruct((1024, 1152...  12.4 us

profile of v8, /device:TPU:1, one launch (start us, length us, event | category | flops | bytes accessed | tf_op | source)
XLA Modules:
  0.0 44.5 jit_solution(2413170652983157187)
XLA Ops:
  0.6 12.4 %planes.1 = (bf16[1024,1152]{1,0:T(8,128)(2,1)S(1)}, f32[512,128]{1,0:T(8,128)S(1)}, bf16[2,4,64,128]{3,2,1,0:T(8,128)(2,1)S(1)}, bf16[3456,128]{1,0:T(8,128)(2,...) custom-call(bf16[8,64,128]{2,1,0:T(8,128)(2,1)} %bitcast.6, bf16[8,64,128]{2,1,0:T(8,128)(2,1)} %bitcast.7, ...), custom_call_target="tpu_custom_call" | custom-call | tf_op jit(solution)/shard_map/planes/pallas_call | solution.py:534
  13.0 30.8 %whole_step.1 = (bf16[8,64,128]{2,1,0:T(8,128)(2,1)S(1)}, f32[118,128]{1,0:T(8,128)S(1)}) custom-call(bf16[1024,1152]{1,0:T(8,128)(2,1)S(1)} %get-tuple-element.12.refs_0_, f32[512,128]{1,0:T(8,128)S(1)} %get-tuple-element.13.refs_1_, bf16[2,4,64,128]{3,2,1,0:T(8,128)(2,1)S(1)} %get-tuple-element.14.refs_2_, ...), custom_call_target="tpu_custom_call" | custom-call | tf_op jit(solution)/shard_map/whole_step/pallas_call | solution.py:558
  43.8 0.7 %store.1 = (bf16[8,64,128]{2,1,0:T(8,128)(2,1)}, f32[118,128]{1,0:T(8,128)}) custom-call(bf16[8,64,128]{2,1,0:T(8,128)(2,1)S(1)} %get-tuple-element.18.grad_input_ref, f32[118,128]{1,0:T(8,128)S(1)} %get-tuple-element.19.share_ref), custom_call_target="tpu_custom_call" | custom-call | tf_op jit(solution)/shard_map/store/pallas_call | solution.py:593

commit v9 on v8

--- a/solution.py
+++ b/solution.py
@@ -180,7 +180,7 @@
 
 def planes_kernel(
     inputs_ref, cotangent_ref, w_conv_any, w_down_any, w_up_any, columns, middle, upstream, w_conv, w_down, w_up,
-    field, load_sem, near_send, near_recv, low_recv, high_recv,
+    order, back, twice, field, load_sem, near_send, near_recv, low_recv, high_recv,
 ):
     sp = lax.axis_index("sp")
     dp = lax.axis_index("dp")
@@ -249,6 +249,7 @@
     def _():
         field[3] = jnp.zeros((4, 64, 128), BF)
 
+    order_matrices(order, back, twice)
     for load in loads:
         load.wait()
     group_wait(field.at[0], near_recv.at[0])
@@ -278,9 +279,9 @@
 
 def step_kernel(
     scale,
-    planes, middle, upstream, w_conv, w_down, w_up,
+    planes, middle, upstream, w_conv, w_down, w_up, order, back, twice,
     grad_input_ref, share_ref,
-    w_flip, columns, turned, slope, order, back, twice, rows,
+    w_flip, columns, turned, slope, rows,
     grad_field, grad_out,
     pair_in, pair_sum, first_in, first_sum, second_in, second_sum, z_in, final,
     own_sem, halo_send, halo_low, halo_high, grad_send, grad_recv,
@@ -394,7 +395,6 @@
     def _():
         grad_field[3] = jnp.zeros((4, 64, 128), BF)
 
-    order_matrices(order, back, twice)
     pre_conv = middle[...] + tap_dot(planes, w_conv, 0)
     pre_conv += tap_dot(planes, w_conv, 2)
     hidden, pre_slope = logistic_parts(pre_conv)
@@ -531,7 +531,7 @@
 
     dma = pltpu.SemaphoreType.DMA
     vmem = pltpu.VMEM
-    planes, middle, upstream, w_conv, w_down, w_up = pl.pallas_call(
+    held = pl.pallas_call(
         planes_kernel,
         out_shape=(
             jax.ShapeDtypeStruct((1024, 1152), BF),
@@ -540,9 +540,12 @@
             jax.ShapeDtypeStruct((3456, 128), BF),
             jax.ShapeDtypeStruct((1024, 256), BF),
             jax.ShapeDtypeStruct((2048, 128), BF),
+            jax.ShapeDtypeStruct((128, 128), BF),
+            jax.ShapeDtypeStruct((128, 128), BF),
+            jax.ShapeDtypeStruct((128, 256), BF),
         ),
         in_specs=[pl.BlockSpec(memory_space=pl.ANY)] * 5,
-        out_specs=(pl.BlockSpec(memory_space=vmem),) * 6,
+        out_specs=(pl.BlockSpec(memory_space=vmem),) * 9,
         scratch_shapes=[vmem((4, 4, 64, 128), BF), dma((5,)), dma((4,)), dma((2,)), dma, dma],
         compiler_params=pltpu.CompilerParams(
             collective_id=0, has_side_effects=True, vmem_limit_bytes=16 * 1024 * 1024
@@ -561,16 +564,13 @@
             jax.ShapeDtypeStruct((8, 64, 128), BF),
             jax.ShapeDtypeStruct((SHARE, 128), F32),
         ),
-        in_specs=[pl.BlockSpec(memory_space=vmem)] * 6,
+        in_specs=[pl.BlockSpec(memory_space=vmem)] * 9,
         out_specs=(pl.BlockSpec(memory_space=vmem), pl.BlockSpec(memory_space=vmem)),
         scratch_shapes=[
             vmem((3456, 128), BF),
             vmem((1024, 1152), BF),
             vmem((1152, 1024), BF),
             vmem((512, 128), F32),
-            vmem((128, 128), BF),
-            vmem((128, 128), BF),
-            vmem((128, 256), BF),
             vmem((16, TILES, 8, 128), BF),
             vmem((4, 4, 64, 128), BF),
             vmem((2, 4, 64, 128), BF),
@@ -589,7 +589,7 @@
             collective_id=1, has_side_effects=True, vmem_limit_bytes=48 * 1024 * 1024
         ),
         name="whole_step",
-    )(planes, middle, upstream, w_conv, w_down, w_up)
+    )(*held)
     grad_input, share = pl.pallas_call(
         store_kernel,
         out_shape=(

time: 44.7 us -> 44.2 us (0.989)
  Pallas kernels: 43.9 us -> 43.4 us
    pallas_call x1, Pallas kernels: 30.8 us -> 30.3 us  [per_device(): pl.pallas_call(kernel, out_shape=(jax.ShapeDtypeStruct((8, 64, 128), BF),...]
where the time goes in v9:
time: 44.2 us; the launch traced here: 44 us
  Pallas kernels  43.4 us (98%)
  between operations  0.65 us (1%)
    pallas_call x1, Pallas kernels, per_device(): pl.pallas_call(kernel, out_shape=(jax.ShapeDtypeStruct((8, 64, 128), BF),...  30.3 us
    pallas_call x1, Pallas kernels, per_device(): pl.pallas_call(planes_kernel, out_shape=(jax.ShapeDtypeStruct((1024, 1152...  12.4 us

profile of v9, /device:TPU:1, one launch (start us, length us, event | category | flops | bytes accessed | tf_op | source)
XLA Modules:
  0.0 44.0 jit_solution(3006453658775357214)
XLA Ops:
  0.6 12.4 %planes.1 = (bf16[1024,1152]{1,0:T(8,128)(2,1)S(1)}, f32[512,128]{1,0:T(8,128)S(1)}, bf16[2,4,64,128]{3,2,1,0:T(8,128)(2,1)S(1)}, bf16[3456,128]{1,0:T(8,128)(2,...) custom-call(bf16[8,64,128]{2,1,0:T(8,128)(2,1)} %bitcast.6, ...), custom_call_target="tpu_custom_call" | custom-call | tf_op jit(solution)/shard_map/planes/pallas_call | solution.py:534
  13.0 30.3 %whole_step.1 = (bf16[8,64,128]{2,1,0:T(8,128)(2,1)S(1)}, f32[118,128]{1,0:T(8,128)S(1)}) custom-call(bf16[1024,1152]{1,0:T(8,128)(2,1)S(1)} %get-tuple-element.15.refs_0_, f32[512,128]{1,0:T(8,128)S(1)} %get-tuple-element.16.refs_1_, bf16[2,4,64,128]{3,2,1,0:T(8,128)(2,1)S(1)} %get-tuple-element.17.refs_2_, ...), custom_call_target="tpu_custom_call" | custom-call | tf_op jit(solution)/shard_map/whole_step/pallas_call | solution.py:561
  43.4 0.7 %store.1 = (bf16[8,64,128]{2,1,0:T(8,128)(2,1)}, f32[118,128]{1,0:T(8,128)}) custom-call(bf16[8,64,128]{2,1,0:T(8,128)(2,1)S(1)} %get-tuple-element.24.grad_input_ref, f32[118,128]{1,0:T(8,128)S(1)} %get-tuple-element.25.share_ref), custom_call_target="tpu_custom_call" | custom-call | tf_op jit(solution)/shard_map/store/pallas_call | solution.py:593
